TPU v7x, 512 devices: a whole 4x4x16 slice. The times are simulated.
512 devices in a mesh: section: 8 (over z_hi, x), dp: 64 (over y, z_lo, core).
Axes of the slice: x: 4, y: 4, z: 16 (z_hi: 2, z_lo: 8; z = z_hi * 8 + z_lo), core: 2. Of those that a mesh axis runs over, the one named last changes fastest.
Arguments:
- clips: bfloat16 [128, 8, 2, 8, 256], P('dp'), may hold values from -6 to 6
- cotangent: bfloat16 [128, 8, 2, 8, 256], P('dp'), may hold values from -6 to 6
- spatial_kernel: bfloat16 [8, 2304, 256], P('section'), may hold values from -0.125 to 0.125
- temporal_kernel: bfloat16 [8, 768, 256], P('section'), may hold values from -0.21875 to 0.21875
Outputs:
- grad_spatial: float32 [8, 2304, 256], P('section', 'dp')
- grad_temporal: float32 [8, 768, 256], P('section', 'dp')
All inputs are finite; a program needn't handle non-finite values.
Results may differ from a plain program's by a relative error of at most 0.024.
Values may be sent and summed in bfloat16 or wider, within the bound.
A program may use at most 64 MiB of HBM per device.

v0:
```python
import math

import jax
import jax.numpy as jnp
from jax import lax
from jax.sharding import PartitionSpec as P


def passed_along(array, axis, by):
    devices = lax.axis_size(axis)
    pairs = [(i, i + by) for i in range(devices) if 0 <= i + by < devices]
    return lax.ppermute(array, axis, pairs)


def offset_cells(values, axis_no, offset):
    if offset == 0:
        return values
    length = values.shape[axis_no]
    padding = [(0, 0)] * values.ndim
    if offset > 0:
        padding[axis_no] = (0, offset)
        return lax.slice_in_dim(jnp.pad(values, padding), offset, offset + length, axis=axis_no)
    padding[axis_no] = (-offset, 0)
    return lax.slice_in_dim(jnp.pad(values, padding), 0, length, axis=axis_no)


def space_patches(x_tile):
    pieces = [
        offset_cells(offset_cells(x_tile, 1, row_off), 2, col_off)
        for row_off in (-1, 0, 1)
        for col_off in (-1, 0, 1)
    ]
    return jnp.concatenate(pieces, axis=-1).reshape(-1, 9 * x_tile.shape[-1])


def time_patches(h_tile):
    pieces = [offset_cells(h_tile, 0, shift_by) for shift_by in (-1, 0, 1)]
    return jnp.concatenate(pieces, axis=-1).reshape(-1, 3 * h_tile.shape[-1])


def contract_rows(left, right):
    return lax.dot_general(
        left, right, (((0,), (0,)), ((), ())), preferred_element_type=jnp.float32
    )


def against_rows(left, right):
    return lax.dot_general(
        left, right, (((1,), (1,)), ((), ())), preferred_element_type=jnp.float32
    )


def section_forward(x_tile, w_space, w_time):
    shape = x_tile.shape
    channels = shape[-1]
    p_space = space_patches(x_tile)
    pre_act = jnp.dot(p_space, w_space, preferred_element_type=jnp.float32)
    hidden = jax.nn.silu(pre_act).astype(jnp.bfloat16)
    p_time = time_patches(hidden.reshape(shape))
    branch = jnp.dot(p_time, w_time, preferred_element_type=jnp.float32)
    return (
        (x_tile.reshape(-1, channels).astype(jnp.float32) + branch)
        .astype(jnp.bfloat16)
        .reshape(shape)
    )


def section_backward(x_tile, g_tile, w_space, w_time):
    shape = x_tile.shape
    channels = shape[-1]
    p_space = space_patches(x_tile)
    pre_act = jnp.dot(p_space, w_space, preferred_element_type=jnp.float32)
    hidden = jax.nn.silu(pre_act).astype(jnp.bfloat16)
    p_time = time_patches(hidden.reshape(shape))
    g_out = g_tile.reshape(-1, channels)
    g_ptime = against_rows(g_out, w_time)
    g_hidden = jnp.zeros(shape, jnp.float32)
    for index, shift_by in enumerate((-1, 0, 1)):
        piece = g_ptime[:, index * channels : (index + 1) * channels].reshape(shape)
        g_hidden = g_hidden + offset_cells(piece, 0, -shift_by)
    sigma = jax.nn.sigmoid(pre_act)
    g_pre = (g_hidden.reshape(-1, channels) * sigma * (1.0 + pre_act * (1.0 - sigma))).astype(
        jnp.bfloat16
    )
    g_pspace = against_rows(g_pre, w_space)
    g_conv = jnp.zeros(shape, jnp.float32)
    index = 0
    for row_off in (-1, 0, 1):
        for col_off in (-1, 0, 1):
            piece = g_pspace[:, index * channels : (index + 1) * channels].reshape(shape)
            g_conv = g_conv + offset_cells(offset_cells(piece, 1, -row_off), 2, -col_off)
            index = index + 1
    g_in = (g_tile.astype(jnp.float32) + g_conv).astype(jnp.bfloat16)
    return (g_in, p_space, p_time, g_pre, g_out)


def body(clips, cotangent, spatial_kernel, temporal_kernel):
    w_space = spatial_kernel[0]
    w_time = temporal_kernel[0]
    sections = lax.axis_size("section")
    place = lax.axis_index("section")
    micro = clips.shape[0]
    tile = clips.shape[1:]
    cells = tile[0] * tile[1] * tile[2]
    rounds = micro + sections - 1
    scale = 1.0 / math.sqrt(micro * lax.axis_size("dp") * cells)

    def forward_round(moment, carry):
        incoming, saved = carry
        which = moment - place
        live = jnp.logical_and(which >= 0, which < micro)
        slot = jnp.clip(which, 0, micro - 1)
        fresh = lax.dynamic_index_in_dim(clips, jnp.minimum(moment, micro - 1), 0, keepdims=False)
        x_tile = jnp.where(place == 0, fresh, incoming)
        result = lax.cond(
            live, lambda tile_in: section_forward(tile_in, w_space, w_time), jnp.zeros_like, x_tile
        )
        kept = lax.dynamic_index_in_dim(saved, slot, 0, keepdims=False)
        saved = lax.dynamic_update_index_in_dim(saved, jnp.where(live, x_tile, kept), slot, 0)
        return (passed_along(result, "section", 1), saved)

    start_fwd = (jnp.zeros(tile, jnp.bfloat16), jnp.zeros(clips.shape, jnp.bfloat16))
    unused, saved = lax.fori_loop(0, rounds, forward_round, start_fwd)

    def arriving(moment, incoming):
        which = moment - (sections - 1 - place)
        live = jnp.logical_and(which >= 0, which < micro)
        slot = jnp.clip(which, 0, micro - 1)
        fresh = lax.dynamic_index_in_dim(
            cotangent, jnp.clip(moment, 0, micro - 1), 0, keepdims=False
        )
        g_tile = jnp.where(place == sections - 1, fresh, incoming)
        x_tile = lax.dynamic_index_in_dim(saved, slot, 0, keepdims=False)
        return (live, slot, x_tile, g_tile)

    def send_back(g_in):
        return passed_along(g_in, "section", -1)

    def backward_round(moment, carry):
        incoming, sum_space, sum_time = carry
        live, slot, x_tile, g_tile = arriving(moment, incoming)

        def active(operands):
            g_in, p_space, p_time, g_pre, g_out = section_backward(
                operands[0], operands[1], w_space, w_time
            )
            return (g_in, contract_rows(p_space, g_pre), contract_rows(p_time, g_out))

        def resting(operands):
            return (
                jnp.zeros_like(operands[1]),
                jnp.zeros_like(sum_space),
                jnp.zeros_like(sum_time),
            )

        g_in, add_space, add_time = lax.cond(live, active, resting, (x_tile, g_tile))
        return (send_back(g_in), sum_space + add_space, sum_time + add_time)

    start_bwd = (
        jnp.zeros(tile, jnp.bfloat16),
        jnp.zeros(w_space.shape, jnp.float32),
        jnp.zeros(w_time.shape, jnp.float32),
    )
    unused, sum_space, sum_time = lax.fori_loop(0, rounds, backward_round, start_bwd)
    grad_space, grad_time = (
        lax.psum_scatter(sum_space * scale, "dp", scatter_dimension=0, tiled=True),
        lax.psum_scatter(sum_time * scale, "dp", scatter_dimension=0, tiled=True),
    )
    return (grad_space[None], grad_time[None])


def solution(mesh):
    return jax.shard_map(
        body,
        mesh=mesh,
        in_specs=(
            P("dp", None, None, None, None),
            P("dp", None, None, None, None),
            P("section", None, None),
            P("section", None, None),
        ),
        out_specs=(P("section", "dp", None), P("section", "dp", None)),
        check_vma=False,
    )
```

profile of v0, /device:TPU:15, one launch (start us, length us, event | category | flops | bytes accessed | tf_op | source)
XLA Modules:
  0.0 662.4 jit_solution(15662328524616935787)
XLA Ops:
  1.3 168.8 %while.36 = (s32[]{:T(128)}, bf16[8,2,8,256]{3,2,1,0:T(8,128)(2,1)S(1)}, bf16[2,8,2,8,256]{4,3,2,1,0:T(8,128)(2,1)}, s32[]{:T(128)}, pred[]{:T(512)}, /*index=5*...) while((s32[]{:T(128)}, ...), condition=%wide.region_3.4_spmd, body=%wide.region_0.3_spmd.sunk | while | flops 202244112 | bytes 6423370 | solution.py:123
  3.7 15.4 %collective-permute-start = (bf16[8,2,8,256]{3,2,1,0:T(8,128)(2,1)S(1)}, bf16[8,2,8,256]{3,2,1,0:T(8,128)(2,1)S(1)}, u32[]{:S(2)}, u32[]{:S(2)}) collective-permute-start(bf16[8,2,8,256]{3,2,1,0:T(8,128)(2,1)S(1)} %get-tuple-element.799), channel_id=1, source_target_pairs={{0,64},{64,128},{128,192},{192,256},{256,320},{320,384},{384,448},... | collective-permute-start | bytes 196616 | tf_op jit(solution)/shard_map/while/body/eval_jaxpr/ppermute | solution.py:12
  22.8 14.6 %collective-permute-start = (bf16[8,2,8,256]{3,2,1,0:T(8,128)(2,1)S(1)}, bf16[8,2,8,256]{3,2,1,0:T(8,128)(2,1)S(1)}, u32[]{:S(2)}, u32[]{:S(2)}) collective-permute-start(bf16[8,2,8,256]{3,2,1,0:T(8,128)(2,1)S(1)} %get-tuple-element.799), channel_id=1, source_target_pairs={{0,64},{64,128},{128,192},{192,256},{256,320},{320,384},{384,448},... | collective-permute-start | bytes 196616 | tf_op jit(solution)/shard_map/while/body/eval_jaxpr/ppermute | solution.py:12
  41.0 14.6 %collective-permute-start = (bf16[8,2,8,256]{3,2,1,0:T(8,128)(2,1)S(1)}, bf16[8,2,8,256]{3,2,1,0:T(8,128)(2,1)S(1)}, u32[]{:S(2)}, u32[]{:S(2)}) collective-permute-start(bf16[8,2,8,256]{3,2,1,0:T(8,128)(2,1)S(1)} %get-tuple-element.799), channel_id=1, source_target_pairs={{0,64},{64,128},{128,192},{192,256},{256,320},{320,384},{384,448},... | collective-permute-start | bytes 196616 | tf_op jit(solution)/shard_map/while/body/eval_jaxpr/ppermute | solution.py:12
  61.3 12.4 %collective-permute-start = (bf16[8,2,8,256]{3,2,1,0:T(8,128)(2,1)S(1)}, bf16[8,2,8,256]{3,2,1,0:T(8,128)(2,1)S(1)}, u32[]{:S(2)}, u32[]{:S(2)}) collective-permute-start(bf16[8,2,8,256]{3,2,1,0:T(8,128)(2,1)S(1)} %get-tuple-element.799), channel_id=1, source_target_pairs={{0,64},{64,128},{128,192},{192,256},{256,320},{320,384},{384,448},... | collective-permute-start | bytes 196616 | tf_op jit(solution)/shard_map/while/body/eval_jaxpr/ppermute | solution.py:12
  79.5 14.5 %collective-permute-start = (bf16[8,2,8,256]{3,2,1,0:T(8,128)(2,1)S(1)}, bf16[8,2,8,256]{3,2,1,0:T(8,128)(2,1)S(1)}, u32[]{:S(2)}, u32[]{:S(2)}) collective-permute-start(bf16[8,2,8,256]{3,2,1,0:T(8,128)(2,1)S(1)} %get-tuple-element.799), channel_id=1, source_target_pairs={{0,64},{64,128},{128,192},{192,256},{256,320},{320,384},{384,448},... | collective-permute-start | bytes 196616 | tf_op jit(solution)/shard_map/while/body/eval_jaxpr/ppermute | solution.py:12
  97.7 16.6 %collective-permute-start = (bf16[8,2,8,256]{3,2,1,0:T(8,128)(2,1)S(1)}, bf16[8,2,8,256]{3,2,1,0:T(8,128)(2,1)S(1)}, u32[]{:S(2)}, u32[]{:S(2)}) collective-permute-start(bf16[8,2,8,256]{3,2,1,0:T(8,128)(2,1)S(1)} %get-tuple-element.799), channel_id=1, source_target_pairs={{0,64},{64,128},{128,192},{192,256},{256,320},{320,384},{384,448},... | collective-permute-start | bytes 196616 | tf_op jit(solution)/shard_map/while/body/eval_jaxpr/ppermute | solution.py:12
  118.0 14.5 %collective-permute-start = (bf16[8,2,8,256]{3,2,1,0:T(8,128)(2,1)S(1)}, bf16[8,2,8,256]{3,2,1,0:T(8,128)(2,1)S(1)}, u32[]{:S(2)}, u32[]{:S(2)}) collective-permute-start(bf16[8,2,8,256]{3,2,1,0:T(8,128)(2,1)S(1)} %get-tuple-element.799), channel_id=1, source_target_pairs={{0,64},{64,128},{128,192},{192,256},{256,320},{320,384},{384,448},... | collective-permute-start | bytes 196616 | tf_op jit(solution)/shard_map/while/body/eval_jaxpr/ppermute | solution.py:12
  136.1 14.5 %collective-permute-start = (bf16[8,2,8,256]{3,2,1,0:T(8,128)(2,1)S(1)}, bf16[8,2,8,256]{3,2,1,0:T(8,128)(2,1)S(1)}, u32[]{:S(2)}, u32[]{:S(2)}) collective-permute-start(bf16[8,2,8,256]{3,2,1,0:T(8,128)(2,1)S(1)} %get-tuple-element.799), channel_id=1, source_target_pairs={{0,64},{64,128},{128,192},{192,256},{256,320},{320,384},{384,448},... | collective-permute-start | bytes 196616 | tf_op jit(solution)/shard_map/while/body/eval_jaxpr/ppermute | solution.py:12
  154.3 14.5 %collective-permute-start = (bf16[8,2,8,256]{3,2,1,0:T(8,128)(2,1)S(1)}, bf16[8,2,8,256]{3,2,1,0:T(8,128)(2,1)S(1)}, u32[]{:S(2)}, u32[]{:S(2)}) collective-permute-start(bf16[8,2,8,256]{3,2,1,0:T(8,128)(2,1)S(1)} %get-tuple-element.799), channel_id=1, source_target_pairs={{0,64},{64,128},{128,192},{192,256},{256,320},{320,384},{384,448},... | collective-permute-start | bytes 196616 | tf_op jit(solution)/shard_map/while/body/eval_jaxpr/ppermute | solution.py:12
  170.2 155.8 %while.37 = (s32[]{:T(128)}, bf16[8,2,8,256]{3,2,1,0:T(8,128)(2,1)S(1)}, f32[2304,256]{1,0:T(8,128)}, f32[768,256]{1,0:T(8,128)}, s32[]{:T(128)}, /*index=5*/pre...) while((s32[]{:T(128)}, ...), condition=%wide.region_7.8_spmd.clone, body=%wide.region_4.7_spmd.clone.sunk | while | flops 556630016 | bytes 43385328 | solution.py:164
  175.1 11.5 %collective-permute-done.1 = bf16[8,2,8,256]{3,2,1,0:T(8,128)(2,1)S(1)} collective-permute-done((bf16[8,2,8,256]{3,2,1,0:T(8,128)(2,1)S(1)}, bf16[8,2,8,256]{3,2,1,0:T(8,128)(2,1)S(1)}, u32[]{:S(2)}, u32[]{:S(2)}) %collective-permute-start.1) | collective-permute-done | bytes 65568 | tf_op jit(solution)/shard_map/while/body/eval_jaxpr/ppermute | solution.py:12
  188.8 3.4 select_add_fusion.4
  194.3 8.4 %collective-permute-done.1 = bf16[8,2,8,256]{3,2,1,0:T(8,128)(2,1)S(1)} collective-permute-done((bf16[8,2,8,256]{3,2,1,0:T(8,128)(2,1)S(1)}, bf16[8,2,8,256]{3,2,1,0:T(8,128)(2,1)S(1)}, u32[]{:S(2)}, u32[]{:S(2)}) %collective-permute-start.1) | collective-permute-done | bytes 65568 | tf_op jit(solution)/shard_map/while/body/eval_jaxpr/ppermute | solution.py:12
  204.8 3.4 select_add_fusion.4
  210.4 8.4 %collective-permute-done.1 = bf16[8,2,8,256]{3,2,1,0:T(8,128)(2,1)S(1)} collective-permute-done((bf16[8,2,8,256]{3,2,1,0:T(8,128)(2,1)S(1)}, bf16[8,2,8,256]{3,2,1,0:T(8,128)(2,1)S(1)}, u32[]{:S(2)}, u32[]{:S(2)}) %collective-permute-start.1) | collective-permute-done | bytes 65568 | tf_op jit(solution)/shard_map/while/body/eval_jaxpr/ppermute | solution.py:12
  226.5 8.5 %collective-permute-done.1 = bf16[8,2,8,256]{3,2,1,0:T(8,128)(2,1)S(1)} collective-permute-done((bf16[8,2,8,256]{3,2,1,0:T(8,128)(2,1)S(1)}, bf16[8,2,8,256]{3,2,1,0:T(8,128)(2,1)S(1)}, u32[]{:S(2)}, u32[]{:S(2)}) %collective-permute-start.1) | collective-permute-done | bytes 65568 | tf_op jit(solution)/shard_map/while/body/eval_jaxpr/ppermute | solution.py:12
  234.9 5.4 conditional.6
  247.8 8.4 %collective-permute-done.1 = bf16[8,2,8,256]{3,2,1,0:T(8,128)(2,1)S(1)} collective-permute-done((bf16[8,2,8,256]{3,2,1,0:T(8,128)(2,1)S(1)}, bf16[8,2,8,256]{3,2,1,0:T(8,128)(2,1)S(1)}, u32[]{:S(2)}, u32[]{:S(2)}) %collective-permute-start.1) | collective-permute-done | bytes 65568 | tf_op jit(solution)/shard_map/while/body/eval_jaxpr/ppermute | solution.py:12
  256.2 5.4 conditional.6
  269.0 8.4 %collective-permute-done.1 = bf16[8,2,8,256]{3,2,1,0:T(8,128)(2,1)S(1)} collective-permute-done((bf16[8,2,8,256]{3,2,1,0:T(8,128)(2,1)S(1)}, bf16[8,2,8,256]{3,2,1,0:T(8,128)(2,1)S(1)}, u32[]{:S(2)}, u32[]{:S(2)}) %collective-permute-start.1) | collective-permute-done | bytes 65568 | tf_op jit(solution)/shard_map/while/body/eval_jaxpr/ppermute | solution.py:12
  285.1 8.7 %collective-permute-done.1 = bf16[8,2,8,256]{3,2,1,0:T(8,128)(2,1)S(1)} collective-permute-done((bf16[8,2,8,256]{3,2,1,0:T(8,128)(2,1)S(1)}, bf16[8,2,8,256]{3,2,1,0:T(8,128)(2,1)S(1)}, u32[]{:S(2)}, u32[]{:S(2)}) %collective-permute-start.1) | collective-permute-done | bytes 65568 | tf_op jit(solution)/shard_map/while/body/eval_jaxpr/ppermute | solution.py:12
  301.5 8.4 %collective-permute-done.1 = bf16[8,2,8,256]{3,2,1,0:T(8,128)(2,1)S(1)} collective-permute-done((bf16[8,2,8,256]{3,2,1,0:T(8,128)(2,1)S(1)}, bf16[8,2,8,256]{3,2,1,0:T(8,128)(2,1)S(1)}, u32[]{:S(2)}, u32[]{:S(2)}) %collective-permute-start.1) | collective-permute-done | bytes 65568 | tf_op jit(solution)/shard_map/while/body/eval_jaxpr/ppermute | solution.py:12
  317.6 8.4 %collective-permute-done.1 = bf16[8,2,8,256]{3,2,1,0:T(8,128)(2,1)S(1)} collective-permute-done((bf16[8,2,8,256]{3,2,1,0:T(8,128)(2,1)S(1)}, bf16[8,2,8,256]{3,2,1,0:T(8,128)(2,1)S(1)}, u32[]{:S(2)}, u32[]{:S(2)}) %collective-permute-start.1) | collective-permute-done | bytes 65568 | tf_op jit(solution)/shard_map/while/body/eval_jaxpr/ppermute | solution.py:12
  328.9 232.3 %fusion.35 = (f32[40,256]{1,0:T(8,128)S(1)}, f32[16,256]{1,0:T(8,128)S(1)}) fusion(f32[2304,256]{1,0:T(8,128)S(1)} %broadcast_multiply_fusion, f32[768,256]{1,0:T(8,128)S(1)} %broadcast_multiply_fusion.1), kind=kCustom, calls=%all-reduce-scatter.2 | all-reduce-scatter fusion | flops 917506 | bytes 3205120
  565.1 3.8 collective-permute-start.24
  573.5 11.4 %collective-permute-done.24 = f32[12,256]{1,0:T(8,128)S(1)} collective-permute-done((f32[12,256]{1,0:T(8,128)S(1)}, f32[12,256]{1,0:T(8,128)S(1)}, u32[]{:S(2)}, u32[]{:S(2)}) %collective-permute-start.24) | collective-permute-done | bytes 12320
  589.6 12.7 %collective-permute-start.16 = (f32[16,256]{1,0:T(8,128)S(1)}, f32[16,256]{1,0:T(8,128)S(1)}, u32[]{:S(2)}, u32[]{:S(2)}) collective-permute-start(f32[16,256]{1,0:T(8,128)S(1)} %get-tuple-element.568), channel_id=1, source_target_pairs={{0,8},{1,9},{2,10},{3,11},{4,12},{5,13},{6,14},{7,15},{8,16},{9,17... | collective-permute-start | bytes 49160
  605.2 5.3 collective-permute-start.2
  619.6 5.9 collective-permute-start.22
  637.9 5.8 collective-permute-start.5
  651.7 6.3 collective-permute-done.6
  (259 shorter events, 164.7 us)
Async XLA Ops:
  3.7 16.7 %collective-permute-start = (bf16[8,2,8,256]{3,2,1,0:T(8,128)(2,1)S(1)}, bf16[8,2,8,256]{3,2,1,0:T(8,128)(2,1)S(1)}, u32[]{:S(2)}, u32[]{:S(2)}) collective-permute-start(bf16[8,2,8,256]{3,2,1,0:T(8,128)(2,1)S(1)} %get-tuple-element.799), channel_id=1, source_target_pairs={{0,64},{64,128},{128,192},{192,256},{256,320},{320,384},{384,448},... | collective-permute-start | bytes 196616 | tf_op jit(solution)/shard_map/while/body/eval_jaxpr/ppermute | solution.py:12
  22.8 15.9 %collective-permute-start = (bf16[8,2,8,256]{3,2,1,0:T(8,128)(2,1)S(1)}, bf16[8,2,8,256]{3,2,1,0:T(8,128)(2,1)S(1)}, u32[]{:S(2)}, u32[]{:S(2)}) collective-permute-start(bf16[8,2,8,256]{3,2,1,0:T(8,128)(2,1)S(1)} %get-tuple-element.799), channel_id=1, source_target_pairs={{0,64},{64,128},{128,192},{192,256},{256,320},{320,384},{384,448},... | collective-permute-start | bytes 196616 | tf_op jit(solution)/shard_map/while/body/eval_jaxpr/ppermute | solution.py:12
  41.0 15.9 %collective-permute-start = (bf16[8,2,8,256]{3,2,1,0:T(8,128)(2,1)S(1)}, bf16[8,2,8,256]{3,2,1,0:T(8,128)(2,1)S(1)}, u32[]{:S(2)}, u32[]{:S(2)}) collective-permute-start(bf16[8,2,8,256]{3,2,1,0:T(8,128)(2,1)S(1)} %get-tuple-element.799), channel_id=1, source_target_pairs={{0,64},{64,128},{128,192},{192,256},{256,320},{320,384},{384,448},... | collective-permute-start | bytes 196616 | tf_op jit(solution)/shard_map/while/body/eval_jaxpr/ppermute | solution.py:12
  61.3 13.7 %collective-permute-start = (bf16[8,2,8,256]{3,2,1,0:T(8,128)(2,1)S(1)}, bf16[8,2,8,256]{3,2,1,0:T(8,128)(2,1)S(1)}, u32[]{:S(2)}, u32[]{:S(2)}) collective-permute-start(bf16[8,2,8,256]{3,2,1,0:T(8,128)(2,1)S(1)} %get-tuple-element.799), channel_id=1, source_target_pairs={{0,64},{64,128},{128,192},{192,256},{256,320},{320,384},{384,448},... | collective-permute-start | bytes 196616 | tf_op jit(solution)/shard_map/while/body/eval_jaxpr/ppermute | solution.py:12
  79.5 15.8 %collective-permute-start = (bf16[8,2,8,256]{3,2,1,0:T(8,128)(2,1)S(1)}, bf16[8,2,8,256]{3,2,1,0:T(8,128)(2,1)S(1)}, u32[]{:S(2)}, u32[]{:S(2)}) collective-permute-start(bf16[8,2,8,256]{3,2,1,0:T(8,128)(2,1)S(1)} %get-tuple-element.799), channel_id=1, source_target_pairs={{0,64},{64,128},{128,192},{192,256},{256,320},{320,384},{384,448},... | collective-permute-start | bytes 196616 | tf_op jit(solution)/shard_map/while/body/eval_jaxpr/ppermute | solution.py:12
  97.7 17.9 %collective-permute-start = (bf16[8,2,8,256]{3,2,1,0:T(8,128)(2,1)S(1)}, bf16[8,2,8,256]{3,2,1,0:T(8,128)(2,1)S(1)}, u32[]{:S(2)}, u32[]{:S(2)}) collective-permute-start(bf16[8,2,8,256]{3,2,1,0:T(8,128)(2,1)S(1)} %get-tuple-element.799), channel_id=1, source_target_pairs={{0,64},{64,128},{128,192},{192,256},{256,320},{320,384},{384,448},... | collective-permute-start | bytes 196616 | tf_op jit(solution)/shard_map/while/body/eval_jaxpr/ppermute | solution.py:12
  118.0 15.8 %collective-permute-start = (bf16[8,2,8,256]{3,2,1,0:T(8,128)(2,1)S(1)}, bf16[8,2,8,256]{3,2,1,0:T(8,128)(2,1)S(1)}, u32[]{:S(2)}, u32[]{:S(2)}) collective-permute-start(bf16[8,2,8,256]{3,2,1,0:T(8,128)(2,1)S(1)} %get-tuple-element.799), channel_id=1, source_target_pairs={{0,64},{64,128},{128,192},{192,256},{256,320},{320,384},{384,448},... | collective-permute-start | bytes 196616 | tf_op jit(solution)/shard_map/while/body/eval_jaxpr/ppermute | solution.py:12
  136.1 15.8 %collective-permute-start = (bf16[8,2,8,256]{3,2,1,0:T(8,128)(2,1)S(1)}, bf16[8,2,8,256]{3,2,1,0:T(8,128)(2,1)S(1)}, u32[]{:S(2)}, u32[]{:S(2)}) collective-permute-start(bf16[8,2,8,256]{3,2,1,0:T(8,128)(2,1)S(1)} %get-tuple-element.799), channel_id=1, source_target_pairs={{0,64},{64,128},{128,192},{192,256},{256,320},{320,384},{384,448},... | collective-permute-start | bytes 196616 | tf_op jit(solution)/shard_map/while/body/eval_jaxpr/ppermute | solution.py:12
  154.3 15.8 %collective-permute-start = (bf16[8,2,8,256]{3,2,1,0:T(8,128)(2,1)S(1)}, bf16[8,2,8,256]{3,2,1,0:T(8,128)(2,1)S(1)}, u32[]{:S(2)}, u32[]{:S(2)}) collective-permute-start(bf16[8,2,8,256]{3,2,1,0:T(8,128)(2,1)S(1)} %get-tuple-element.799), channel_id=1, source_target_pairs={{0,64},{64,128},{128,192},{192,256},{256,320},{320,384},{384,448},... | collective-permute-start | bytes 196616 | tf_op jit(solution)/shard_map/while/body/eval_jaxpr/ppermute | solution.py:12
  170.4 16.2 %collective-permute-start.1 = (bf16[8,2,8,256]{3,2,1,0:T(8,128)(2,1)S(1)}, bf16[8,2,8,256]{3,2,1,0:T(8,128)(2,1)S(1)}, u32[]{:S(2)}, u32[]{:S(2)}) collective-permute-start(bf16[8,2,8,256]{3,2,1,0:T(8,128)(2,1)S(1)} %get-tuple-element.718), channel_id=1, source_target_pairs={{64,0},{128,64},{192,128},{256,192},{320,256},{384,320},{448,384},... | collective-permute-start | bytes 196616 | tf_op jit(solution)/shard_map/while/body/eval_jaxpr/ppermute | solution.py:12
  186.8 15.8 %collective-permute-start.1 = (bf16[8,2,8,256]{3,2,1,0:T(8,128)(2,1)S(1)}, bf16[8,2,8,256]{3,2,1,0:T(8,128)(2,1)S(1)}, u32[]{:S(2)}, u32[]{:S(2)}) collective-permute-start(bf16[8,2,8,256]{3,2,1,0:T(8,128)(2,1)S(1)} %get-tuple-element.718), channel_id=1, source_target_pairs={{64,0},{128,64},{192,128},{256,192},{320,256},{384,320},{448,384},... | collective-permute-start | bytes 196616 | tf_op jit(solution)/shard_map/while/body/eval_jaxpr/ppermute | solution.py:12
  202.9 15.8 %collective-permute-start.1 = (bf16[8,2,8,256]{3,2,1,0:T(8,128)(2,1)S(1)}, bf16[8,2,8,256]{3,2,1,0:T(8,128)(2,1)S(1)}, u32[]{:S(2)}, u32[]{:S(2)}) collective-permute-start(bf16[8,2,8,256]{3,2,1,0:T(8,128)(2,1)S(1)} %get-tuple-element.718), channel_id=1, source_target_pairs={{64,0},{128,64},{192,128},{256,192},{320,256},{384,320},{448,384},... | collective-permute-start | bytes 196616 | tf_op jit(solution)/shard_map/while/body/eval_jaxpr/ppermute | solution.py:12
  219.0 15.9 %collective-permute-start.1 = (bf16[8,2,8,256]{3,2,1,0:T(8,128)(2,1)S(1)}, bf16[8,2,8,256]{3,2,1,0:T(8,128)(2,1)S(1)}, u32[]{:S(2)}, u32[]{:S(2)}) collective-permute-start(bf16[8,2,8,256]{3,2,1,0:T(8,128)(2,1)S(1)} %get-tuple-element.718), channel_id=1, source_target_pairs={{64,0},{128,64},{192,128},{256,192},{320,256},{384,320},{448,384},... | collective-permute-start | bytes 196616 | tf_op jit(solution)/shard_map/while/body/eval_jaxpr/ppermute | solution.py:12
  240.3 15.9 %collective-permute-start.1 = (bf16[8,2,8,256]{3,2,1,0:T(8,128)(2,1)S(1)}, bf16[8,2,8,256]{3,2,1,0:T(8,128)(2,1)S(1)}, u32[]{:S(2)}, u32[]{:S(2)}) collective-permute-start(bf16[8,2,8,256]{3,2,1,0:T(8,128)(2,1)S(1)} %get-tuple-element.718), channel_id=1, source_target_pairs={{64,0},{128,64},{192,128},{256,192},{320,256},{384,320},{448,384},... | collective-permute-start | bytes 196616 | tf_op jit(solution)/shard_map/while/body/eval_jaxpr/ppermute | solution.py:12
  261.5 15.8 %collective-permute-start.1 = (bf16[8,2,8,256]{3,2,1,0:T(8,128)(2,1)S(1)}, bf16[8,2,8,256]{3,2,1,0:T(8,128)(2,1)S(1)}, u32[]{:S(2)}, u32[]{:S(2)}) collective-permute-start(bf16[8,2,8,256]{3,2,1,0:T(8,128)(2,1)S(1)} %get-tuple-element.718), channel_id=1, source_target_pairs={{64,0},{128,64},{192,128},{256,192},{320,256},{384,320},{448,384},... | collective-permute-start | bytes 196616 | tf_op jit(solution)/shard_map/while/body/eval_jaxpr/ppermute | solution.py:12
  277.6 16.1 %collective-permute-start.1 = (bf16[8,2,8,256]{3,2,1,0:T(8,128)(2,1)S(1)}, bf16[8,2,8,256]{3,2,1,0:T(8,128)(2,1)S(1)}, u32[]{:S(2)}, u32[]{:S(2)}) collective-permute-start(bf16[8,2,8,256]{3,2,1,0:T(8,128)(2,1)S(1)} %get-tuple-element.718), channel_id=1, source_target_pairs={{64,0},{128,64},{192,128},{256,192},{320,256},{384,320},{448,384},... | collective-permute-start | bytes 196616 | tf_op jit(solution)/shard_map/while/body/eval_jaxpr/ppermute | solution.py:12
  294.0 15.8 %collective-permute-start.1 = (bf16[8,2,8,256]{3,2,1,0:T(8,128)(2,1)S(1)}, bf16[8,2,8,256]{3,2,1,0:T(8,128)(2,1)S(1)}, u32[]{:S(2)}, u32[]{:S(2)}) collective-permute-start(bf16[8,2,8,256]{3,2,1,0:T(8,128)(2,1)S(1)} %get-tuple-element.718), channel_id=1, source_target_pairs={{64,0},{128,64},{192,128},{256,192},{320,256},{384,320},{448,384},... | collective-permute-start | bytes 196616 | tf_op jit(solution)/shard_map/while/body/eval_jaxpr/ppermute | solution.py:12
  310.1 15.8 %collective-permute-start.1 = (bf16[8,2,8,256]{3,2,1,0:T(8,128)(2,1)S(1)}, bf16[8,2,8,256]{3,2,1,0:T(8,128)(2,1)S(1)}, u32[]{:S(2)}, u32[]{:S(2)}) collective-permute-start(bf16[8,2,8,256]{3,2,1,0:T(8,128)(2,1)S(1)} %get-tuple-element.718), channel_id=1, source_target_pairs={{64,0},{128,64},{192,128},{256,192},{320,256},{384,320},{448,384},... | collective-permute-start | bytes 196616 | tf_op jit(solution)/shard_map/while/body/eval_jaxpr/ppermute | solution.py:12
  561.2 25.6 %collective-permute-start.10 = (f32[16,256]{1,0:T(8,128)S(1)}, f32[16,256]{1,0:T(8,128)S(1)}, u32[]{:S(2)}, u32[]{:S(2)}) collective-permute-start(f32[16,256]{1,0:T(8,128)S(1)} %get-tuple-element.568), channel_id=1, source_target_pairs={{0,2},{1,3},{2,4},{3,5},{4,6},{5,7},{6,8},{7,9},{8,10},{9,11},{10,... | collective-permute-start | bytes 49160
  563.1 26.4 %collective-permute-start.11 = (f32[16,256]{1,0:T(8,128)S(1)}, f32[16,256]{1,0:T(8,128)S(1)}, u32[]{:S(2)}, u32[]{:S(2)}) collective-permute-start(f32[16,256]{1,0:T(8,128)S(1)} %get-tuple-element.568), channel_id=1, source_target_pairs={{0,3},{1,4},{2,5},{3,6},{4,7},{5,8},{6,9},{7,10},{8,11},{9,12},{10... | collective-permute-start | bytes 49160
  565.1 19.8 %collective-permute-start.24 = (f32[12,256]{1,0:T(8,128)S(1)}, f32[12,256]{1,0:T(8,128)S(1)}, u32[]{:S(2)}, u32[]{:S(2)}) collective-permute-start(f32[12,256]{1,0:T(8,128)S(1)} %slice.231), channel_id=1, source_target_pairs={{0,16},{1,17},{2,18},{3,19},{4,20},{5,21},{6,22},{7,23},{8,24},{9,... | collective-permute-start | bytes 36872
  568.9 33.4 %collective-permute-start.12 = (f32[16,256]{1,0:T(8,128)S(1)}, f32[16,256]{1,0:T(8,128)S(1)}, u32[]{:S(2)}, u32[]{:S(2)}) collective-permute-start(f32[16,256]{1,0:T(8,128)S(1)} %get-tuple-element.568), channel_id=1, source_target_pairs={{0,4},{1,5},{2,6},{3,7},{4,8},{5,9},{6,10},{7,11},{8,12},{9,13},{1... | collective-permute-start | bytes 49160
  570.8 34.3 %collective-permute-start.13 = (f32[16,256]{1,0:T(8,128)S(1)}, f32[16,256]{1,0:T(8,128)S(1)}, u32[]{:S(2)}, u32[]{:S(2)}) collective-permute-start(f32[16,256]{1,0:T(8,128)S(1)} %get-tuple-element.568), channel_id=1, source_target_pairs={{0,5},{1,6},{2,7},{3,8},{4,9},{5,10},{6,11},{7,12},{8,13},{9,14},{... | collective-permute-start | bytes 49160
  584.9 25.6 %collective-permute-start.14 = (f32[16,256]{1,0:T(8,128)S(1)}, f32[16,256]{1,0:T(8,128)S(1)}, u32[]{:S(2)}, u32[]{:S(2)}) collective-permute-start(f32[16,256]{1,0:T(8,128)S(1)} %get-tuple-element.568), channel_id=1, source_target_pairs={{0,6},{1,7},{2,8},{3,9},{4,10},{5,11},{6,12},{7,13},{8,14},{9,15},... | collective-permute-start | bytes 49160
  586.8 26.9 %collective-permute-start.15 = (f32[16,256]{1,0:T(8,128)S(1)}, f32[16,256]{1,0:T(8,128)S(1)}, u32[]{:S(2)}, u32[]{:S(2)}) collective-permute-start(f32[16,256]{1,0:T(8,128)S(1)} %get-tuple-element.568), channel_id=1, source_target_pairs={{0,7},{1,8},{2,9},{3,10},{4,11},{5,12},{6,13},{7,14},{8,15},{9,16}... | collective-permute-start | bytes 49160
  589.6 26.1 %collective-permute-start.16 = (f32[16,256]{1,0:T(8,128)S(1)}, f32[16,256]{1,0:T(8,128)S(1)}, u32[]{:S(2)}, u32[]{:S(2)}) collective-permute-start(f32[16,256]{1,0:T(8,128)S(1)} %get-tuple-element.568), channel_id=1, source_target_pairs={{0,8},{1,9},{2,10},{3,11},{4,12},{5,13},{6,14},{7,15},{8,16},{9,17... | collective-permute-start | bytes 49160
  602.3 15.3 %collective-permute-start.17 = (f32[16,256]{1,0:T(8,128)S(1)}, f32[16,256]{1,0:T(8,128)S(1)}, u32[]{:S(2)}, u32[]{:S(2)}) collective-permute-start(f32[16,256]{1,0:T(8,128)S(1)} %get-tuple-element.568), channel_id=1, source_target_pairs={{0,9},{1,10},{2,11},{3,12},{4,13},{5,14},{6,15},{7,16},{8,17},{9,1... | collective-permute-start | bytes 49160
  605.2 42.9 %collective-permute-start.2 = (f32[40,256]{1,0:T(8,128)S(1)}, f32[40,256]{1,0:T(8,128)S(1)}, u32[]{:S(2)}, u32[]{:S(2)}) collective-permute-start(f32[40,256]{1,0:T(8,128)S(1)} %get-tuple-element.567), channel_id=1, source_target_pairs={{0,1},{1,2},{2,3},{3,4},{4,5},{5,6},{6,7},{7,8},{8,9},{9,10},{10,1... | collective-permute-start | bytes 122888
  629.4 16.2 %collective-permute-start.8 = (f32[12,256]{1,0:T(8,128)S(1)}, f32[12,256]{1,0:T(8,128)S(1)}, u32[]{:S(2)}, u32[]{:S(2)}) collective-permute-start(f32[12,256]{1,0:T(8,128)S(1)} %slice.230), channel_id=1, source_target_pairs={{0,7},{1,8},{2,9},{3,10},{4,11},{5,12},{6,13},{7,14},{8,15},{9,16}... | collective-permute-start | bytes 36872
  633.2 18.5 %collective-permute-start.3 = (f32[40,256]{1,0:T(8,128)S(1)}, f32[40,256]{1,0:T(8,128)S(1)}, u32[]{:S(2)}, u32[]{:S(2)}) collective-permute-start(f32[40,256]{1,0:T(8,128)S(1)} %get-tuple-element.567), channel_id=1, source_target_pairs={{0,2},{1,3},{2,4},{3,5},{4,6},{5,7},{6,8},{7,9},{8,10},{9,11},{10,... | collective-permute-start | bytes 122888
  635.2 16.5 %collective-permute-start.4 = (f32[40,256]{1,0:T(8,128)S(1)}, f32[40,256]{1,0:T(8,128)S(1)}, u32[]{:S(2)}, u32[]{:S(2)}) collective-permute-start(f32[40,256]{1,0:T(8,128)S(1)} %get-tuple-element.567), channel_id=1, source_target_pairs={{0,3},{1,4},{2,5},{3,6},{4,7},{5,8},{6,9},{7,10},{8,11},{9,12},{10... | collective-permute-start | bytes 122888
  637.9 13.8 %collective-permute-start.5 = (f32[40,256]{1,0:T(8,128)S(1)}, f32[40,256]{1,0:T(8,128)S(1)}, u32[]{:S(2)}, u32[]{:S(2)}) collective-permute-start(f32[40,256]{1,0:T(8,128)S(1)} %get-tuple-element.567), channel_id=1, source_target_pairs={{0,4},{1,5},{2,6},{3,7},{4,8},{5,9},{6,10},{7,11},{8,12},{9,13},{1... | collective-permute-start | bytes 122888
  (22 other events, 291.5 us)
where the time goes:
time: 665 us; the launch traced here: 662 us
  blocking collectives  232 us (35%)
  starting transfers between devices  223 us (34%)
  waiting for transfers between devices  111 us (17%)
  other arithmetic  63.8 us (10%)
  local copies, waits for them, and re-layouts  21.5 us (3%)
  matrix products  7.67 us (1%)
    unnamed x1, blocking collectives  232 us
    ppermute x18, starting transfers between devices, passed_along(): return lax.ppermute(array, axis, pairs)  149 us
    ppermute x18, waiting for transfers between devices, passed_along(): return lax.ppermute(array, axis, pairs)  90.6 us
    unnamed x23, starting transfers between devices  74.3 us
    add x18, other arithmetic, backward_round(): return (send_back(g_in), sum_space + add_space, sum_time + add_time)  47.1 us
    unnamed x23, waiting for transfers between devices  20.5 us
    dynamic_update_slice x9, other arithmetic, forward_round(): lax.dynamic_update_index_in_dim(saved, jnp.where(live, x_tile, kept), slo...  13.4 us
  transfers between devices with their start and end apart: 41, of which 21 were waited for; matrix products, arithmetic and copies ran while one was open for 8% of the time, Pallas kernels for 0%

commit v1 on v0

v1 whole, which is shorter than its diff:
```python
import functools
import math

import jax
import jax.numpy as jnp
from jax import lax
from jax.experimental import pallas as pl
from jax.experimental.pallas import tpu as pltpu
from jax.sharding import PartitionSpec as P

MESH = pl.DeviceIdType.MESH
F32 = jnp.float32
BF16 = jnp.bfloat16
C = 256
ROWS = 128
HALF = 64
SPACE = 9 * C
TIME = 3 * C


def by_height(v):
    v = v.astype(F32).reshape(8, 2, 8, C)
    return jnp.concatenate([v[:, 0].reshape(HALF, C), v[:, 1].reshape(HALF, C)], axis=0)


def columns(v):
    w = lax.broadcasted_iota(jnp.int32, v.shape, 0) & 7
    before = jnp.where(w == 0, 0.0, pltpu.roll(v, 1, 0))
    after = jnp.where(w == 7, 0.0, pltpu.roll(v, ROWS - 1, 0))
    return before, after


def frames(v):
    zero = jnp.zeros((8, C), F32)
    before = jnp.concatenate([zero, v[0:56], zero, v[64:120]], axis=0)
    after = jnp.concatenate([v[8:64], zero, v[72:128], zero], axis=0)
    return before, after


def nn(a, b):
    return jnp.dot(a, b, preferred_element_type=F32)


def nt(a, b):
    return lax.dot_general(a, b, (((1,), (1,)), ((), ())), preferred_element_type=F32)


def tn(a, b):
    return lax.dot_general(a, b, (((0,), (0,)), ((), ())), preferred_element_type=F32)


def wide_space(v):
    before, after = columns(v)
    return jnp.concatenate([before, v, after], axis=1).astype(BF16)


def wide_time(v):
    before, after = frames(v)
    return jnp.concatenate([before, v, after], axis=1).astype(BF16)


def space_forward(wide, w):
    same = nn(wide, w[768:1536, :])
    top = nn(wide[HALF:], w[1536:2304, :])
    bottom = nn(wide[:HALF], w[0:768, :])
    return same + jnp.concatenate([top, bottom], axis=0)


def activate(pre):
    sigma = jax.nn.sigmoid(pre)
    hidden = (pre * sigma).astype(BF16).astype(F32)
    return hidden, sigma * (1.0 + pre * (1.0 - sigma))


def g_hidden_of(g, w):
    before, after = frames(g)
    out = nt(after.astype(BF16), w[0:256, :])
    out = out + nt(g.astype(BF16), w[256:512, :])
    return out + nt(before.astype(BF16), w[512:768, :])


def space_backward(g_pre, w):
    before, after = columns(g_pre)
    same = top = bottom = None
    for q, v in enumerate((after, g_pre, before)):
        v = v.astype(BF16)
        a = nt(v, w[768 + 256 * q : 1024 + 256 * q, :])
        t = nt(v[HALF:], w[256 * q : 256 * q + 256, :])
        b = nt(v[:HALF], w[1536 + 256 * q : 1792 + 256 * q, :])
        same, top, bottom = (a, t, b) if same is None else (same + a, top + t, bottom + b)
    return same + jnp.concatenate([top, bottom], axis=0)


def kernel(
    scale,
    clips_ref, cot_ref, ws_ref, wt_ref,
    out_s, out_t,
    wsv, wtv, cl, ct, xin, yout, bx, bg, gin,
    act, bact, xc, hc, gp, gb, dw, part, r1, s1, r2, s2, r3, fin,
    loc, wg_send, wg_recv, wf_send,
    x_send, x_recv, bx_send, bx_recv, ct_send, ct_recv,
    go_send, gin_recv, bg_send, bg_recv,
    r1_sem, r2_send, r2_recv, r3_send, r3_recv, r4_sem,
):
    S = lax.axis_index("section")
    D = lax.axis_index("dp")
    half = S // 4
    x = S % 4
    y = D // 16
    z = (D // 2) % 8
    k = D % 2
    far = D + 8 - 16 * (z // 4)
    sibling = D + 1 - 2 * k
    end = jnp.logical_or(x == 0, x == 3)
    mine = jnp.where(x == 0, 1, 0)
    base = half * 4

    def copy(src, dst, send, recv, section, dp):
        return pltpu.make_async_remote_copy(
            src_ref=src, dst_ref=dst, send_sem=send, recv_sem=recv,
            device_id={"section": section, "dp": dp}, device_id_type=MESH,
        )

    local = [
        pltpu.make_async_copy(clips_ref, cl, loc.at[0]),
        pltpu.make_async_copy(ws_ref, wsv.at[x], loc.at[1]),
        pltpu.make_async_copy(wt_ref, wtv.at[x], loc.at[2]),
    ]
    for c in local:
        c.start()

    barrier = pltpu.get_barrier_semaphore()

    def hello(section, dp):
        pl.semaphore_signal(
            barrier, inc=1, device_id={"section": section, "dp": dp}, device_id_type=MESH
        )

    hello(S, sibling)
    for i in range(1, 4):
        hello(S, lax.rem(y + i, 4) * 16 + lax.rem(D, 16))
        hello(base + lax.rem(x + i, 4), D)
    for i in range(1, 8):
        hello(S, y * 16 + lax.rem(z + i, 8) * 2 + k)

    @pl.when(S == 0)
    def _():
        hello(4, far)

    @pl.when(S == 3)
    def _():
        hello(4, far)
        hello(7, far)

    @pl.when(S == 4)
    def _():
        hello(0, far)
        hello(3, far)

    @pl.when(S == 7)
    def _():
        hello(3, far)

    crossings = jnp.where(end, 1, 0) + jnp.where(jnp.logical_or(S == 3, S == 4), 1, 0)
    pl.semaphore_wait(barrier, 14 + crossings)

    def weight_copies(j, target, slot):
        rows_s = pl.ds(pl.multiple_of(k * 1152, 128), 1152)
        rows_t = pl.ds(pl.multiple_of(k * 384, 128), 384)
        return (
            copy(ws_ref.at[rows_s], wsv.at[j, rows_s], wg_send.at[slot, 0], wg_recv.at[j, k, 0], base + target, D),
            copy(wt_ref.at[rows_t], wtv.at[j, rows_t], wg_send.at[slot, 1], wg_recv.at[j, k, 1], base + target, D),
        )

    def share_copies(j, core):
        rows_s = pl.ds(pl.multiple_of(core * 1152, 128), 1152)
        rows_t = pl.ds(pl.multiple_of(core * 384, 128), 384)
        return (
            copy(wsv.at[j, rows_s], wsv.at[j, rows_s], wf_send.at[j, 0], wg_recv.at[j, core, 0], S, sibling),
            copy(wtv.at[j, rows_t], wtv.at[j, rows_t], wf_send.at[j, 1], wg_recv.at[j, core, 1], S, sibling),
        )

    for slot, target in enumerate((0, 3)):
        @pl.when(x != target)
        def _():
            for c in weight_copies(x, target, slot):
                c.start()

    cot_copy = copy(cot_ref.at[mine], ct, ct_send, ct_recv, S, far)

    @pl.when(jnp.logical_or(S == 4, S == 7))
    def _():
        cot_copy.start()

    for c in local:
        c.wait()

    def rows_of(c, h):
        return pl.ds(pl.multiple_of(h * 128 + c * HALF, HALF), HALF)

    def keep(ref, c, value):
        ref[rows_of(c, 0), :] = value[:HALF]
        ref[rows_of(c, 1), :] = value[HALF:]

    def y_copy(c):
        return copy(yout.at[c], xin.at[c], x_send.at[c], x_recv.at[c], lax.rem(S + 1, 8), D)

    def y_cross(c):
        return copy(yout.at[c], bx.at[0], x_send.at[c], bx_recv, jnp.where(c == 0, 7, 4), far)

    def owner_hidden(c):
        wide = wide_space(xin[c].astype(F32))
        keep(xc, c, wide)
        hidden, slope = activate(space_forward(wide, wsv.at[x]))
        act[c] = slope
        wide = wide_time(hidden)
        keep(hc, c, wide)
        return wide

    @pl.when(half == 0)
    def _():
        def clip(c, carry):
            @pl.when(x == 0)
            def _():
                xin[c] = by_height(cl[c]).astype(BF16)

            @pl.when(x > 0)
            def _():
                y_copy(c).wait_recv()

            wide = owner_hidden(c)
            out = xin[c].astype(F32) + nn(wide, wtv[x])
            yout[c] = out.astype(BF16)

            @pl.when(x < 3)
            def _():
                y_copy(c).start()

            @pl.when(x == 3)
            def _():
                y_cross(c).start()

            return carry

        lax.fori_loop(0, 2, clip, 0)

    def x_copy(j):
        return copy(bx.at[j], xin.at[mine], bx_send.at[j], x_recv.at[mine], base + j, D)

    def g_copy(j):
        return copy(bg.at[j + 1], gin.at[mine], go_send.at[j], gin_recv.at[mine], base + j, D)

    back_copy = copy(bg.at[0], bg.at[4], bg_send, bg_recv, lax.rem(S + 4, 8), far)

    @pl.when(end)
    def _():
        for i in range(1, 4):
            j = lax.rem(x + i, 4)
            for c in weight_copies(j, 0, 0):
                c.wait_recv()
            for c in share_copies(j, k):
                c.start()
        for i in range(1, 4):
            j = lax.rem(x + i, 4)
            for c in share_copies(j, 1 - k):
                c.wait_recv()

        @pl.when(half == 0)
        def _():
            bx[0] = by_height(cl[mine]).astype(BF16)

        @pl.when(half == 1)
        def _():
            y_cross(0).wait_recv()

        def layer(j, carry):
            @pl.when(half == 1)
            def _():
                @pl.when(j == x)
                def _():
                    xin[mine] = bx[j]

                @pl.when(j != x)
                def _():
                    x_copy(j).start()

            v = bx[j].astype(F32)
            hidden, slope = activate(space_forward(wide_space(v), wsv.at[j]))
            bact[j] = slope

            @pl.when(j < 3)
            def _():
                out = v + nn(wide_time(hidden), wtv[j])
                bx[j + 1] = out.astype(BF16)

            return carry

        lax.fori_loop(0, 4, layer, 0)

        @pl.when(half == 0)
        def _():
            back_copy.wait_recv()

        @pl.when(half == 1)
        def _():
            cot_copy.wait_recv()
            bg[4] = by_height(ct[...]).astype(BF16)

        def layer_back(i, carry):
            j = 3 - i

            @pl.when(j == x)
            def _():
                gin[mine] = bg[j + 1]

            @pl.when(j != x)
            def _():
                g_copy(j).start()

            @pl.when(j + half > 0)
            def _():
                g = bg[j + 1].astype(F32)
                g_pre = (g_hidden_of(g, wtv.at[j]) * bact[j]).astype(BF16).astype(F32)
                bg[j] = (g + space_backward(g_pre, wsv.at[j])).astype(BF16)

            return carry

        lax.fori_loop(0, 4, layer_back, 0)

        @pl.when(half == 1)
        def _():
            back_copy.start()

    @pl.when(half == 1)
    def _():
        def clip(c, carry):
            @pl.when(jnp.logical_not(jnp.logical_and(end, c == mine)))
            def _():
                y_copy(c).wait_recv()

            owner_hidden(c)
            return carry

        lax.fori_loop(0, 2, clip, 0)

    def clip_back(i, carry):
        c = jnp.where(i == 0, mine, 1 - mine)

        @pl.when(jnp.logical_not(jnp.logical_and(end, c == mine)))
        def _():
            copy(gin.at[c], gin.at[c], go_send.at[0], gin_recv.at[c], S, D).wait_recv()

        keep(gb, c, gin[c])
        g = gin[c].astype(F32)
        keep(gp, c, (g_hidden_of(g, wtv.at[x]) * act[c]).astype(BF16))
        return carry

    lax.fori_loop(0, 2, clip_back, 0)

    for q in range(3):
        lanes = slice(256 * q, 256 * q + 256)
        dw[SPACE + 256 * q : SPACE + 256 * q + 256, :] = tn(hc[:, lanes], gb[...])
        dw[256 * q : 256 * q + 256, :] = tn(xc[0:128, lanes], gp[128:256, :])
        dw[768 + 256 * q : 1024 + 256 * q, :] = tn(xc[:, lanes], gp[...])
        dw[1536 + 256 * q : 1792 + 256 * q, :] = tn(xc[128:256, lanes], gp[0:128, :])

    def pack(b, carry):
        top = dw[pl.ds(pl.multiple_of(b * 72, 8), 72), :]
        low = dw[pl.ds(pl.multiple_of(SPACE + b * 24, 8), 24), :]
        block = jnp.concatenate([top, low], axis=0).astype(BF16)
        part[0, b // 8, b % 8] = block[:, 0:128]
        part[1, b // 8, b % 8] = block[:, 128:256]
        return carry

    lax.fori_loop(0, 32, pack, 0)

    first = copy(part.at[1 - k], r1, r1_sem.at[0], r1_sem.at[1], S, sibling)
    first.start()
    first.wait_recv()

    def add_cores(b, carry):
        s1[b // 8, b % 8] = (part[k, b // 8, b % 8].astype(F32) + r1[b // 8, b % 8].astype(F32)).astype(BF16)
        return carry

    lax.fori_loop(0, 32, add_cores, 0)

    def y_step(i):
        to = lax.rem(y + i, 4)
        return copy(s1.at[to], r2.at[i - 1], r2_send.at[i - 1], r2_recv.at[i - 1], S, to * 16 + lax.rem(D, 16))

    for i in range(1, 4):
        y_step(i).start()
    for i in range(1, 4):
        y_step(i).wait_recv()

    def add_y(b, carry):
        total = s1[y, b].astype(F32) + r2[0, b].astype(F32) + r2[1, b].astype(F32) + r2[2, b].astype(F32)
        s2[b] = total.astype(BF16)
        return carry

    lax.fori_loop(0, 8, add_y, 0)

    def z_step(i):
        to = lax.rem(z + i, 8)
        return copy(s2.at[to], r3.at[i - 1], r3_send.at[i - 1], r3_recv.at[i - 1], S, y * 16 + to * 2 + k)

    for i in range(1, 8):
        z_step(i).start()
    for i in range(1, 8):
        z_step(i).wait_recv()

    total = s2[z].astype(F32)
    for i in range(7):
        total = total + r3[i].astype(F32)
    fin[k] = total * scale

    final = copy(fin.at[k], fin.at[k], r4_sem.at[0], r4_sem.at[1], S, sibling)
    final.start()
    final.wait_send()
    copy(fin.at[1 - k], fin.at[1 - k], r4_sem.at[0], r4_sem.at[1], S, sibling).wait_recv()

    for core in range(2):
        @pl.when(k == core)
        def _():
            for side in range(2):
                lanes = slice(128 * side, 128 * side + 128)
                out_s[:, lanes] = fin[side, 36 * core : 36 * core + 36, :]
                out_t[:, lanes] = fin[side, 72 + 12 * core : 84 + 12 * core, :]

    first.wait_send()
    for i in range(1, 4):
        y_step(i).wait_send()
    for i in range(1, 8):
        z_step(i).wait_send()
    for slot, target in enumerate((0, 3)):
        @pl.when(x != target)
        def _():
            for c in weight_copies(x, target, slot):
                c.wait_send()

    @pl.when(jnp.logical_or(S == 4, S == 7))
    def _():
        cot_copy.wait_send()

    @pl.when(half == 0)
    def _():
        for c in range(2):
            y_copy(c).wait_send()

    @pl.when(end)
    def _():
        for i in range(1, 4):
            j = lax.rem(x + i, 4)
            for c in share_copies(j, k):
                c.wait_send()
            g_copy(j).wait_send()

            @pl.when(half == 1)
            def _():
                x_copy(j).wait_send()

        @pl.when(half == 1)
        def _():
            back_copy.wait_send()


def body(clips, cotangent, spatial_kernel, temporal_kernel):
    micro = clips.shape[0]
    tile = clips.shape[1:]
    cells = tile[0] * tile[1] * tile[2]
    scale = 1.0 / math.sqrt(micro * lax.axis_size("dp") * cells)
    sem = pltpu.SemaphoreType.DMA
    vmem = pltpu.VMEM
    out_s, out_t = pl.pallas_call(
        functools.partial(kernel, scale),
        out_shape=(jax.ShapeDtypeStruct((36, C), F32), jax.ShapeDtypeStruct((12, C), F32)),
        in_specs=[pl.BlockSpec(memory_space=pl.ANY)] * 4,
        out_specs=(pl.BlockSpec(memory_space=pltpu.VMEM),) * 2,
        scratch_shapes=[
            vmem((4, SPACE, C), BF16),
            vmem((4, TIME, C), BF16),
            vmem((2, ROWS, C), BF16),
            vmem((ROWS, C), BF16),
            vmem((2, ROWS, C), BF16),
            vmem((2, ROWS, C), BF16),
            vmem((4, ROWS, C), BF16),
            vmem((5, ROWS, C), BF16),
            vmem((2, ROWS, C), BF16),
            vmem((2, ROWS, C), F32),
            vmem((4, ROWS, C), F32),
            vmem((2 * ROWS, 3 * C), BF16),
            vmem((2 * ROWS, 3 * C), BF16),
            vmem((2 * ROWS, C), BF16),
            vmem((2 * ROWS, C), BF16),
            vmem((SPACE + TIME, C), F32),
            vmem((2, 4, 8, 96, 128), BF16),
            vmem((4, 8, 96, 128), BF16),
            vmem((4, 8, 96, 128), BF16),
            vmem((3, 8, 96, 128), BF16),
            vmem((8, 96, 128), BF16),
            vmem((7, 96, 128), BF16),
            vmem((2, 96, 128), F32),
            sem((3,)),
            sem((2, 2)),
            sem((4, 2, 2)),
            sem((4, 2)),
            sem((2,)),
            sem((2,)),
            sem((4,)),
            sem,
            sem,
            sem,
            sem((4,)),
            sem((2,)),
            sem,
            sem,
            sem((2,)),
            sem((3,)),
            sem((3,)),
            sem((7,)),
            sem((7,)),
            sem((2,)),
        ],
        compiler_params=pltpu.CompilerParams(
            collective_id=0, has_side_effects=True, vmem_limit_bytes=40 << 20
        ),
        name="window",
    )(
        clips.reshape(micro, cells, tile[3]),
        cotangent.reshape(micro, cells, tile[3]),
        spatial_kernel[0],
        temporal_kernel[0],
    )
    return (out_s[None], out_t[None])


def solution(mesh):
    return jax.shard_map(
        body,
        mesh=mesh,
        in_specs=(
            P("dp", None, None, None, None),
            P("dp", None, None, None, None),
            P("section", None, None),
            P("section", None, None),
        ),
        out_specs=(P("section", "dp", None), P("section", "dp", None)),
        check_vma=False,
    )
```

time: 665 us -> 108 us (0.16)
  the two profiles are of different devices: /device:TPU:15 before, /device:TPU:1 now
where the time goes in v1:
time: 108 us; the launch traced here: 107 us
  Pallas kernels  101 us (94%)
  local copies, waits for them, and re-layouts  5.33 us (5%)
    pallas_call x1, Pallas kernels, body(): pl.pallas_call(functools.partial(kernel, scale), out_shape=(jax.ShapeDtyp...  101 us
    unnamed x10, local copies, waits for them, and re-layouts  5.33 us

profile of v1, /device:TPU:1, one launch (start us, length us, event | category | flops | bytes accessed | tf_op | source)
XLA Modules:
  0.0 107.2 jit_solution(15459420409072569756)
XLA Ops:
  0.6 0.0 copy-start
  0.6 1.3 %copy-done = bf16[1,2304,256]{2,1,0:T(8,128)(2,1)S(1)} copy-done((bf16[1,2304,256]{2,1,0:T(8,128)(2,1)S(1)}, bf16[1,2304,256]{2,1,0:T(8,128)(2,1)}, u32[]{:S(2)}) %copy-start) | copy-done | bytes 1179672
  1.9 0.0 copy-start.1
  1.9 1.0 copy-done.1
  2.9 0.0 copy-start.2
  2.9 0.9 copy-done.2
  3.8 0.0 copy-start.3
  3.8 0.9 copy-done.3
  4.7 101.2 %window.1 = (f32[36,256]{1,0:T(8,128)S(1)}, f32[12,256]{1,0:T(8,128)S(1)}) custom-call(bf16[2,128,256]{2,1,0:T(8,128)(2,1)S(1)} %bitcast.8, bf16[2,128,256]{2,1,0:T(8,128)(2,1)S(1)} %bitcast.9, bf16[2304,256]{1,0:T(8,128)(2,1)S(1)} %bitcast.6, bf16[768,256]{1,0:T(8,128)(2,1)S(1)} %bitcast.7), custom_call_target="tpu_custom_call" | custom-call | tf_op jit(solution)/shard_map/window/pallas_call | solution.py:474
  105.9 0.7 copy.6
  106.6 0.6 copy.7
Async XLA Ops:
  0.6 1.3 %copy-start = (bf16[1,2304,256]{2,1,0:T(8,128)(2,1)S(1)}, bf16[1,2304,256]{2,1,0:T(8,128)(2,1)}, u32[]{:S(2)}) copy-start(bf16[1,2304,256]{2,1,0:T(8,128)(2,1)} %param.6) | copy-start | bytes 3538948
  1.9 1.0 copy-start.1
  2.9 0.9 copy-start.2
  3.8 0.9 copy-start.3

commit v2 on v1

--- a/solution.py
+++ b/solution.py
@@ -97,10 +97,10 @@
     out_s, out_t,
     wsv, wtv, cl, ct, xin, yout, bx, bg, gin,
     act, bact, xc, hc, gp, gb, dw, part, r1, s1, r2, s2, r3, fin,
-    loc, wg_send, wg_recv, wf_send,
+    loc, wg_send, wg_recv, ws_send, ws_recv, wy_send, wy_recv,
     x_send, x_recv, bx_send, bx_recv, ct_send, ct_recv,
     go_send, gin_recv, bg_send, bg_recv,
-    r1_sem, r2_send, r2_recv, r3_send, r3_recv, r4_sem,
+    r1_send, r1_recv, r2_send, r2_recv, r3_send, r3_recv, r4_sem,
 ):
     S = lax.axis_index("section")
     D = lax.axis_index("dp")
@@ -114,6 +114,10 @@
     end = jnp.logical_or(x == 0, x == 3)
     mine = jnp.where(x == 0, 1, 0)
     base = half * 4
+    odd = y % 2
+    lane = lax.rem(D, 16)
+    above = lax.rem(y + 1, 4) * 16 + lane
+    below = lax.rem(y + 3, 4) * 16 + lane
 
     def copy(src, dst, send, recv, section, dp):
         return pltpu.make_async_remote_copy(
@@ -164,27 +168,42 @@
     crossings = jnp.where(end, 1, 0) + jnp.where(jnp.logical_or(S == 3, S == 4), 1, 0)
     pl.semaphore_wait(barrier, 14 + crossings)
 
+    near = jnp.where(x % 2 == 1, 0, 3)
+
+    def both(j, eighth, eighths, send, recv, section, dp, source=None):
+        copies = []
+        for i, (out, held) in enumerate(((ws_ref, wsv), (wt_ref, wtv))):
+            step = held.shape[1] // 8
+            rows = pl.ds(pl.multiple_of(eighth * step, 32), eighths * step)
+            src = held.at[j, rows] if source is None else out.at[rows]
+            copies.append(copy(src, held.at[j, rows], send.at[i], recv.at[i], section, dp))
+        return copies
+
     def weight_copies(j, target, slot):
-        rows_s = pl.ds(pl.multiple_of(k * 1152, 128), 1152)
-        rows_t = pl.ds(pl.multiple_of(k * 384, 128), 384)
-        return (
-            copy(ws_ref.at[rows_s], wsv.at[j, rows_s], wg_send.at[slot, 0], wg_recv.at[j, k, 0], base + target, D),
-            copy(wt_ref.at[rows_t], wtv.at[j, rows_t], wg_send.at[slot, 1], wg_recv.at[j, k, 1], base + target, D),
+        return both(j, 4 * odd + 2 * k, 2, wg_send.at[slot], wg_recv.at[j], base + target, D, "out")
+
+    def share_copies(j, i, core):
+        if i == 0:
+            return both(j, 4 * odd + 2 * core, 2, ws_send.at[j, 0], ws_recv.at[j, 0], S, sibling)
+        return both(j, 4 - 4 * odd + 2 * core + i - 1, 1, ws_send.at[j, i], ws_recv.at[j, i], S, sibling)
+
+    def y_copies(j, i, parity):
+        return both(
+            j, 4 * parity + 2 * k + i, 1, wy_send.at[j, i], wy_recv.at[j, i], S, above if i else below
         )
 
-    def share_copies(j, core):
-        rows_s = pl.ds(pl.multiple_of(core * 1152, 128), 1152)
-        rows_t = pl.ds(pl.multiple_of(core * 384, 128), 384)
-        return (
-            copy(wsv.at[j, rows_s], wsv.at[j, rows_s], wf_send.at[j, 0], wg_recv.at[j, core, 0], S, sibling),
-            copy(wtv.at[j, rows_t], wtv.at[j, rows_t], wf_send.at[j, 1], wg_recv.at[j, core, 1], S, sibling),
-        )
-
-    for slot, target in enumerate((0, 3)):
-        @pl.when(x != target)
-        def _():
-            for c in weight_copies(x, target, slot):
+    def send_weights():
+        for c in weight_copies(x, near, 0):
+            c.start()
+
+        @pl.when(jnp.logical_not(end))
+        def _():
+            for c in weight_copies(x, 3 - near, 1):
                 c.start()
+
+    @pl.when(half == 1)
+    def _():
+        send_weights()
 
     cot_copy = copy(cot_ref.at[mine], ct, ct_send, ct_recv, S, far)
 
@@ -243,6 +262,7 @@
             return carry
 
         lax.fori_loop(0, 2, clip, 0)
+        send_weights()
 
     def x_copy(j):
         return copy(bx.at[j], xin.at[mine], bx_send.at[j], x_recv.at[mine], base + j, D)
@@ -254,16 +274,22 @@
 
     @pl.when(end)
     def _():
-        for i in range(1, 4):
-            j = lax.rem(x + i, 4)
+        others = [jnp.where(x == 0, a, b) for a, b in ((1, 2), (3, 0), (2, 1))]
+        for j in others:
             for c in weight_copies(j, 0, 0):
                 c.wait_recv()
-            for c in share_copies(j, k):
+            for c in y_copies(j, 0, odd) + y_copies(j, 1, odd) + share_copies(j, 0, k):
                 c.start()
-        for i in range(1, 4):
-            j = lax.rem(x + i, 4)
-            for c in share_copies(j, 1 - k):
-                c.wait_recv()
+        for j in others:
+            for i in range(2):
+                for c in y_copies(j, i, 1 - odd):
+                    c.wait_recv()
+                for c in share_copies(j, i + 1, k):
+                    c.start()
+        for j in others:
+            for i in range(3):
+                for c in share_copies(j, i, 1 - k):
+                    c.wait_recv()
 
         @pl.when(half == 0)
         def _():
@@ -364,37 +390,62 @@
         dw[768 + 256 * q : 1024 + 256 * q, :] = tn(xc[:, lanes], gp[...])
         dw[1536 + 256 * q : 1792 + 256 * q, :] = tn(xc[128:256, lanes], gp[0:128, :])
 
-    def pack(b, carry):
-        top = dw[pl.ds(pl.multiple_of(b * 72, 8), 72), :]
-        low = dw[pl.ds(pl.multiple_of(SPACE + b * 24, 8), 24), :]
-        block = jnp.concatenate([top, low], axis=0).astype(BF16)
-        part[0, b // 8, b % 8] = block[:, 0:128]
-        part[1, b // 8, b % 8] = block[:, 128:256]
+    ahead = jnp.where(odd == k, 1, 3)
+    blocks = [lax.rem(y + i, 4) for i in (2, 1, 3, 0)]
+    forth = lax.rem(y + ahead, 4)
+    back = lax.rem(y + 4 - ahead, 4)
+
+    def core_step(i, column):
+        yb = blocks[i]
+        return copy(part.at[column, yb], r1.at[yb], r1_send.at[i], r1_recv.at[i], S, sibling)
+
+    for i in range(4):
+        def pack(b, carry):
+            n = blocks[i] * 8 + b
+            top = dw[pl.ds(pl.multiple_of(n * 72, 8), 72), :]
+            low = dw[pl.ds(pl.multiple_of(SPACE + n * 24, 8), 24), :]
+            block = jnp.concatenate([top, low], axis=0).astype(BF16)
+            part[0, blocks[i], b] = block[:, 0:128]
+            part[1, blocks[i], b] = block[:, 128:256]
+            return carry
+
+        lax.fori_loop(0, 8, pack, 0)
+        core_step(i, 1 - k).start()
+
+    def add_cores(yb):
+        def one(b, carry):
+            s1[yb, b] = (part[k, yb, b].astype(F32) + r1[yb, b].astype(F32)).astype(BF16)
+            return carry
+
+        lax.fori_loop(0, 8, one, 0)
+
+    def y_step(i):
+        return copy(
+            s1.at[(blocks[0], forth, back)[i]], r2.at[i], r2_send.at[i], r2_recv.at[i],
+            S, (forth, forth, back)[i] * 16 + lane,
+        )
+
+    core_step(0, k).wait_recv()
+    add_cores(blocks[0])
+    y_step(0).start()
+    core_step(1, k).wait_recv()
+    core_step(2, k).wait_recv()
+    add_cores(forth)
+    y_step(1).start()
+    y_step(0).wait_recv()
+
+    def add_relayed(b, carry):
+        total = part[k, back, b].astype(F32) + r1[back, b].astype(F32) + r2[0, b].astype(F32)
+        s1[back, b] = total.astype(BF16)
         return carry
 
-    lax.fori_loop(0, 32, pack, 0)
-
-    first = copy(part.at[1 - k], r1, r1_sem.at[0], r1_sem.at[1], S, sibling)
-    first.start()
-    first.wait_recv()
-
-    def add_cores(b, carry):
-        s1[b // 8, b % 8] = (part[k, b // 8, b % 8].astype(F32) + r1[b // 8, b % 8].astype(F32)).astype(BF16)
-        return carry
-
-    lax.fori_loop(0, 32, add_cores, 0)
-
-    def y_step(i):
-        to = lax.rem(y + i, 4)
-        return copy(s1.at[to], r2.at[i - 1], r2_send.at[i - 1], r2_recv.at[i - 1], S, to * 16 + lax.rem(D, 16))
-
-    for i in range(1, 4):
-        y_step(i).start()
-    for i in range(1, 4):
-        y_step(i).wait_recv()
-
+    lax.fori_loop(0, 8, add_relayed, 0)
+    y_step(2).start()
+    core_step(3, k).wait_recv()
+    y_step(1).wait_recv()
+    y_step(2).wait_recv()
     def add_y(b, carry):
-        total = s1[y, b].astype(F32) + r2[0, b].astype(F32) + r2[1, b].astype(F32) + r2[2, b].astype(F32)
+        total = part[k, y, b].astype(F32) + r1[y, b].astype(F32) + r2[1, b].astype(F32) + r2[2, b].astype(F32)
         s2[b] = total.astype(BF16)
         return carry
 
@@ -427,16 +478,19 @@
                 out_s[:, lanes] = fin[side, 36 * core : 36 * core + 36, :]
                 out_t[:, lanes] = fin[side, 72 + 12 * core : 84 + 12 * core, :]
 
-    first.wait_send()
-    for i in range(1, 4):
+    for i in range(4):
+        core_step(i, 1 - k).wait_send()
+    for i in range(3):
         y_step(i).wait_send()
     for i in range(1, 8):
         z_step(i).wait_send()
-    for slot, target in enumerate((0, 3)):
-        @pl.when(x != target)
-        def _():
-            for c in weight_copies(x, target, slot):
-                c.wait_send()
+    for c in weight_copies(x, near, 0):
+        c.wait_send()
+
+    @pl.when(jnp.logical_not(end))
+    def _():
+        for c in weight_copies(x, 3 - near, 1):
+            c.wait_send()
 
     @pl.when(jnp.logical_or(S == 4, S == 7))
     def _():
@@ -451,8 +505,11 @@
     def _():
         for i in range(1, 4):
             j = lax.rem(x + i, 4)
-            for c in share_copies(j, k):
+            for c in y_copies(j, 0, odd) + y_copies(j, 1, odd):
                 c.wait_send()
+            for n in range(3):
+                for c in share_copies(j, n, k):
+                    c.wait_send()
             g_copy(j).wait_send()
 
             @pl.when(half == 1)
@@ -474,7 +531,7 @@
     out_s, out_t = pl.pallas_call(
         functools.partial(kernel, scale),
         out_shape=(jax.ShapeDtypeStruct((36, C), F32), jax.ShapeDtypeStruct((12, C), F32)),
-        in_specs=[pl.BlockSpec(memory_space=pl.ANY)] * 4,
+        in_specs=[pl.BlockSpec(memory_space=pltpu.HBM)] * 4,
         out_specs=(pl.BlockSpec(memory_space=pltpu.VMEM),) * 2,
         scratch_shapes=[
             vmem((4, SPACE, C), BF16),
@@ -502,8 +559,11 @@
             vmem((2, 96, 128), F32),
             sem((3,)),
             sem((2, 2)),
+            sem((4, 2)),
+            sem((4, 3, 2)),
+            sem((4, 3, 2)),
             sem((4, 2, 2)),
-            sem((4, 2)),
+            sem((4, 2, 2)),
             sem((2,)),
             sem((2,)),
             sem((4,)),
@@ -514,7 +574,8 @@
             sem((2,)),
             sem,
             sem,
-            sem((2,)),
+            sem((4,)),
+            sem((4,)),
             sem((3,)),
             sem((3,)),
             sem((7,)),
@@ -522,7 +583,7 @@
             sem((2,)),
         ],
         compiler_params=pltpu.CompilerParams(
-            collective_id=0, has_side_effects=True, vmem_limit_bytes=40 << 20
+            collective_id=0, has_side_effects=True, vmem_limit_bytes=66_900_000
         ),
         name="window",
     )(

time: 108 us -> 88.8 us (0.82)
  Pallas kernels: 101 us -> 85.2 us
  local copies, waits for them, and re-layouts: 5.33 us -> 2.76 us
    pallas_call x1, Pallas kernels: 101 us -> 85.2 us  [body(): pl.pallas_call(functools.partial(kernel, scale), out_shape=(jax.ShapeDtyp...]
    unnamed x10 -> x2, local copies, waits for them, and re-layouts: 5.33 us -> 2.76 us
where the time goes in v2:
time: 88.8 us; the launch traced here: 88.6 us
  Pallas kernels  85.2 us (96%)
  local copies, waits for them, and re-layouts  2.76 us (3%)
    pallas_call x1, Pallas kernels, body(): pl.pallas_call(functools.partial(kernel, scale), out_shape=(jax.ShapeDtyp...  85.2 us
    unnamed x2, local copies, waits for them, and re-layouts  2.76 us

profile of v2, /device:TPU:1, one launch (start us, length us, event | category | flops | bytes accessed | tf_op | source)
XLA Modules:
  0.0 88.6 jit_solution(1763310928548238989)
XLA Ops:
  0.6 85.2 %window.1 = (f32[36,256]{1,0:T(8,128)}, f32[12,256]{1,0:T(8,128)}) custom-call(bf16[2,128,256]{2,1,0:T(8,128)(2,1)} %bitcast.8, bf16[2,128,256]{2,1,0:T(8,128)(2,1)} %bitcast.9, bf16[2304,256]{1,0:T(8,128)(2,1)} %bitcast.6, bf16[768,256]{1,0:T(8,128)(2,1)} %bitcast.7), custom_call_target="tpu_custom_call" | custom-call | tf_op jit(solution)/shard_map/window/pallas_call | solution.py:531
  85.8 1.4 %copy.6 = f32[1,36,256]{2,0,1:T(1,128)} copy(f32[1,36,256]{2,1,0:T(8,128)} %bitcast.10) | data formatting | bytes 73728
  87.2 1.3 %copy.7 = f32[1,12,256]{2,0,1:T(1,128)} copy(f32[1,12,256]{2,1,0:T(8,128)} %bitcast.11) | data formatting | bytes 24576

commit v3 on v2

--- a/solution.py
+++ b/solution.py
@@ -192,18 +192,37 @@
             j, 4 * parity + 2 * k + i, 1, wy_send.at[j, i], wy_recv.at[j, i], S, above if i else below
         )
 
-    def send_weights():
+    passed = jnp.where(x % 2 == 0, 1, 2)
+    passes = jnp.where(end, k == 0, k == 1)
+    middle = jnp.logical_and(jnp.logical_not(end), k == 1)
+
+    def pass_copies():
+        return both(passed, 4 * odd + 2 * k, 2, wg_send.at[2], wg_recv.at[passed], base + near, D)
+
+    def send_near():
         for c in weight_copies(x, near, 0):
             c.start()
 
-        @pl.when(jnp.logical_not(end))
-        def _():
-            for c in weight_copies(x, 3 - near, 1):
+    def pass_middle():
+        @pl.when(middle)
+        def _():
+            for c in weight_copies(passed, near, 0):
+                c.wait_recv()
+            for c in pass_copies():
                 c.start()
 
+    @pl.when(S != 2)
+    def _():
+        send_near()
+
+    @pl.when(middle)
+    def _():
+        for c in weight_copies(x, 3 - x, 1):
+            c.start()
+
     @pl.when(half == 1)
     def _():
-        send_weights()
+        pass_middle()
 
     cot_copy = copy(cot_ref.at[mine], ct, ct_send, ct_recv, S, far)
 
@@ -262,7 +281,12 @@
             return carry
 
         lax.fori_loop(0, 2, clip, 0)
-        send_weights()
+
+        @pl.when(x == 2)
+        def _():
+            send_near()
+
+        pass_middle()
 
     def x_copy(j):
         return copy(bx.at[j], xin.at[mine], bx_send.at[j], x_recv.at[mine], base + j, D)
@@ -274,12 +298,18 @@
 
     @pl.when(end)
     def _():
-        others = [jnp.where(x == 0, a, b) for a, b in ((1, 2), (3, 0), (2, 1))]
+        others = [jnp.where(x == 0, a, b) for a, b in ((1, 0), (3, 2), (2, 1))]
         for j in others:
             for c in weight_copies(j, 0, 0):
                 c.wait_recv()
             for c in y_copies(j, 0, odd) + y_copies(j, 1, odd) + share_copies(j, 0, k):
                 c.start()
+
+            @pl.when(jnp.logical_and(j == passed, k == 0))
+            def _():
+                for c in pass_copies():
+                    c.start()
+
         for j in others:
             for i in range(2):
                 for c in y_copies(j, i, 1 - odd):
@@ -487,9 +517,14 @@
     for c in weight_copies(x, near, 0):
         c.wait_send()
 
-    @pl.when(jnp.logical_not(end))
-    def _():
-        for c in weight_copies(x, 3 - near, 1):
+    @pl.when(middle)
+    def _():
+        for c in weight_copies(x, 3 - x, 1):
+            c.wait_send()
+
+    @pl.when(passes)
+    def _():
+        for c in pass_copies():
             c.wait_send()
 
     @pl.when(jnp.logical_or(S == 4, S == 7))
@@ -558,7 +593,7 @@
             vmem((7, 96, 128), BF16),
             vmem((2, 96, 128), F32),
             sem((3,)),
-            sem((2, 2)),
+            sem((3, 2)),
             sem((4, 2)),
             sem((4, 3, 2)),
             sem((4, 3, 2)),

time: 88.8 us -> 87.5 us (0.985)
  Pallas kernels: 85.2 us -> 83.8 us
    pallas_call x1, Pallas kernels: 85.2 us -> 83.8 us  [body(): pl.pallas_call(functools.partial(kernel, scale), out_shape=(jax.ShapeDtyp...]
where the time goes in v3:
time: 87.5 us; the launch traced here: 87.2 us
  Pallas kernels  83.8 us (96%)
  local copies, waits for them, and re-layouts  2.76 us (3%)
    pallas_call x1, Pallas kernels, body(): pl.pallas_call(functools.partial(kernel, scale), out_shape=(jax.ShapeDtyp...  83.8 us
    unnamed x2, local copies, waits for them, and re-layouts  2.76 us

profile of v3, /device:TPU:1, one launch (start us, length us, event | category | flops | bytes accessed | tf_op | source)
XLA Modules:
  0.0 87.2 jit_solution(16252147662947825439)
XLA Ops:
  0.6 83.8 %window.1 = (f32[36,256]{1,0:T(8,128)}, f32[12,256]{1,0:T(8,128)}) custom-call(bf16[2,128,256]{2,1,0:T(8,128)(2,1)} %bitcast.8, bf16[2,128,256]{2,1,0:T(8,128)(2,1)} %bitcast.9, bf16[2304,256]{1,0:T(8,128)(2,1)} %bitcast.6, bf16[768,256]{1,0:T(8,128)(2,1)} %bitcast.7), custom_call_target="tpu_custom_call" | custom-call | tf_op jit(solution)/shard_map/window/pallas_call | solution.py:566
  84.5 1.4 %copy.6 = f32[1,36,256]{2,0,1:T(1,128)} copy(f32[1,36,256]{2,1,0:T(8,128)} %bitcast.10) | data formatting | bytes 73728
  85.9 1.3 %copy.7 = f32[1,12,256]{2,0,1:T(1,128)} copy(f32[1,12,256]{2,1,0:T(8,128)} %bitcast.11) | data formatting | bytes 24576

commit v4 on v2

--- a/solution.py
+++ b/solution.py
@@ -74,9 +74,9 @@
 
 def g_hidden_of(g, w):
     before, after = frames(g)
-    out = nt(after.astype(BF16), w[0:256, :])
-    out = out + nt(g.astype(BF16), w[256:512, :])
-    return out + nt(before.astype(BF16), w[512:768, :])
+    out = nt(after.astype(BF16), w[SPACE : SPACE + 256, :])
+    out = out + nt(g.astype(BF16), w[SPACE + 256 : SPACE + 512, :])
+    return out + nt(before.astype(BF16), w[SPACE + 512 : SPACE + 768, :])
 
 
 def space_backward(g_pre, w):
@@ -95,7 +95,7 @@
     scale,
     clips_ref, cot_ref, ws_ref, wt_ref,
     out_s, out_t,
-    wsv, wtv, cl, ct, xin, yout, bx, bg, gin,
+    wv, cl, ct, xin, yout, bx, bg, gin,
     act, bact, xc, hc, gp, gb, dw, part, r1, s1, r2, s2, r3, fin,
     loc, wg_send, wg_recv, ws_send, ws_recv, wy_send, wy_recv,
     x_send, x_recv, bx_send, bx_recv, ct_send, ct_recv,
@@ -127,8 +127,8 @@
 
     local = [
         pltpu.make_async_copy(clips_ref, cl, loc.at[0]),
-        pltpu.make_async_copy(ws_ref, wsv.at[x], loc.at[1]),
-        pltpu.make_async_copy(wt_ref, wtv.at[x], loc.at[2]),
+        pltpu.make_async_copy(ws_ref, wv.at[x, 0:SPACE], loc.at[1]),
+        pltpu.make_async_copy(wt_ref, wv.at[x, SPACE : SPACE + TIME], loc.at[2]),
     ]
     for c in local:
         c.start()
@@ -168,51 +168,79 @@
     crossings = jnp.where(end, 1, 0) + jnp.where(jnp.logical_or(S == 3, S == 4), 1, 0)
     pl.semaphore_wait(barrier, 14 + crossings)
 
-    near = jnp.where(x % 2 == 1, 0, 3)
-
-    def both(j, eighth, eighths, send, recv, section, dp, source=None):
-        copies = []
-        for i, (out, held) in enumerate(((ws_ref, wsv), (wt_ref, wtv))):
-            step = held.shape[1] // 8
-            rows = pl.ds(pl.multiple_of(eighth * step, 32), eighths * step)
-            src = held.at[j, rows] if source is None else out.at[rows]
-            copies.append(copy(src, held.at[j, rows], send.at[i], recv.at[i], section, dp))
-        return copies
-
-    def weight_copies(j, target, slot):
-        return both(j, 4 * odd + 2 * k, 2, wg_send.at[slot], wg_recv.at[j], base + target, D, "out")
-
-    def share_copies(j, i, core):
-        if i == 0:
-            return both(j, 4 * odd + 2 * core, 2, ws_send.at[j, 0], ws_recv.at[j, 0], S, sibling)
-        return both(j, 4 - 4 * odd + 2 * core + i - 1, 1, ws_send.at[j, i], ws_recv.at[j, i], S, sibling)
-
-    def y_copies(j, i, parity):
-        return both(
-            j, 4 * parity + 2 * k + i, 1, wy_send.at[j, i], wy_recv.at[j, i], S, above if i else below
-        )
-
-    def send_weights():
-        for c in weight_copies(x, near, 0):
-            c.start()
-
-        @pl.when(jnp.logical_not(end))
-        def _():
-            for c in weight_copies(x, 3 - near, 1):
-                c.start()
-
-    @pl.when(half == 1)
-    def _():
-        send_weights()
-
-    cot_copy = copy(cot_ref.at[mine], ct, ct_send, ct_recv, S, far)
-
-    @pl.when(jnp.logical_or(S == 4, S == 7))
-    def _():
-        cot_copy.start()
-
     for c in local:
         c.wait()
+
+    near = jnp.where(x % 2 == 1, 0, 3)
+    passed = jnp.where(x % 2 == 0, 1, 2)
+    other = jnp.where(x == 0, 3, 0)
+    distant = jnp.where(x == 0, 2, 1)
+    middle = jnp.logical_and(jnp.logical_not(end), k == 1)
+    passes = jnp.logical_or(middle, jnp.logical_and(end, k == 0))
+
+    def chunk_copy(j, c, parity, core, send, recv, section, dp):
+        n = 8 * parity + 4 * core + 2 * (c % 2) + c // 2
+        rows = pl.ds(pl.multiple_of(n * 192, 192), 192)
+        return copy(wv.at[j, rows], wv.at[j, rows], send, recv, section, dp)
+
+    def x_chunk(j, c, target, slot):
+        return chunk_copy(j, c, odd, k, wg_send.at[slot, c], wg_recv.at[j, c], base + target, D)
+
+    def y_chunk(j, c, parity):
+        dp = jnp.where(c % 2 == 1, above, below)
+        return chunk_copy(j, c, parity, k, wy_send.at[j, c], wy_recv.at[j, c], S, dp)
+
+    def core_chunk(j, c, far_rows, core):
+        parity = 1 - odd if far_rows else odd
+        at = 4 * far_rows + c
+        return chunk_copy(j, c, parity, core, ws_send.at[j, at], ws_recv.at[j, at], S, sibling)
+
+    def each(body):
+        def step(c, carry):
+            body(c)
+            return carry
+
+        lax.fori_loop(0, 4, step, 0)
+
+    def take_x(j, c):
+        x_chunk(j, c, 0, 0).wait_recv()
+        y_chunk(j, c, odd).start()
+
+        @pl.when(jnp.logical_and(j == passed, k == 0))
+        def _():
+            x_chunk(j, c, near, 2).start()
+
+        core_chunk(j, c, 0, k).start()
+
+    def take_y(j, c):
+        y_chunk(j, c, 1 - odd).wait_recv()
+        core_chunk(j, c, 1, k).start()
+
+    def pass_middle():
+        @pl.when(middle)
+        def _():
+            @each
+            def _(c):
+                x_chunk(passed, c, 0, 0).wait_recv()
+                x_chunk(passed, c, near, 2).start()
+
+    @each
+    def _(c):
+        x_chunk(x, c, near, 0).start()
+
+        @pl.when(middle)
+        def _():
+            x_chunk(x, c, 3 - x, 1).start()
+
+    cot_copy = copy(cot_ref.at[mine], ct, ct_send, ct_recv, S, far)
+
+    @pl.when(jnp.logical_or(S == 4, S == 7))
+    def _():
+        cot_copy.start()
+
+    @pl.when(half == 1)
+    def _():
+        pass_middle()
 
     def rows_of(c, h):
         return pl.ds(pl.multiple_of(h * 128 + c * HALF, HALF), HALF)
@@ -230,39 +258,51 @@
     def owner_hidden(c):
         wide = wide_space(xin[c].astype(F32))
         keep(xc, c, wide)
-        hidden, slope = activate(space_forward(wide, wsv.at[x]))
+        hidden, slope = activate(space_forward(wide, wv.at[x]))
         act[c] = slope
         wide = wide_time(hidden)
         keep(hc, c, wide)
         return wide
 
-    @pl.when(half == 0)
-    def _():
+    def forward(first):
         def clip(c, carry):
-            @pl.when(x == 0)
-            def _():
+            if first:
                 xin[c] = by_height(cl[c]).astype(BF16)
-
-            @pl.when(x > 0)
-            def _():
+            else:
                 y_copy(c).wait_recv()
-
             wide = owner_hidden(c)
-            out = xin[c].astype(F32) + nn(wide, wtv[x])
+            out = xin[c].astype(F32) + nn(wide, wv[x, SPACE : SPACE + TIME, :])
             yout[c] = out.astype(BF16)
-
-            @pl.when(x < 3)
-            def _():
+            if first:
                 y_copy(c).start()
-
-            @pl.when(x == 3)
-            def _():
-                y_cross(c).start()
+            else:
+                @pl.when(x < 3)
+                def _():
+                    y_copy(c).start()
+
+                @pl.when(x == 3)
+                def _():
+                    y_cross(c).start()
 
             return carry
 
         lax.fori_loop(0, 2, clip, 0)
-        send_weights()
+
+    @pl.when(S == 0)
+    def _():
+        forward(True)
+
+    @pl.when(end)
+    def _():
+        @each
+        def _(c):
+            take_x(passed, c)
+            take_x(other, c)
+
+    @pl.when(jnp.logical_and(half == 0, x > 0))
+    def _():
+        forward(False)
+        pass_middle()
 
     def x_copy(j):
         return copy(bx.at[j], xin.at[mine], bx_send.at[j], x_recv.at[mine], base + j, D)
@@ -274,22 +314,19 @@
 
     @pl.when(end)
     def _():
-        others = [jnp.where(x == 0, a, b) for a, b in ((1, 2), (3, 0), (2, 1))]
-        for j in others:
-            for c in weight_copies(j, 0, 0):
-                c.wait_recv()
-            for c in y_copies(j, 0, odd) + y_copies(j, 1, odd) + share_copies(j, 0, k):
-                c.start()
-        for j in others:
-            for i in range(2):
-                for c in y_copies(j, i, 1 - odd):
-                    c.wait_recv()
-                for c in share_copies(j, i + 1, k):
-                    c.start()
-        for j in others:
-            for i in range(3):
-                for c in share_copies(j, i, 1 - k):
-                    c.wait_recv()
+        @each
+        def _(c):
+            take_x(distant, c)
+            take_y(passed, c)
+            take_y(other, c)
+        @each
+        def _(c):
+            take_y(distant, c)
+        @each
+        def _(c):
+            for j in (passed, other, distant):
+                core_chunk(j, c, 0, 1 - k).wait_recv()
+                core_chunk(j, c, 1, 1 - k).wait_recv()
 
         @pl.when(half == 0)
         def _():
@@ -311,12 +348,12 @@
                     x_copy(j).start()
 
             v = bx[j].astype(F32)
-            hidden, slope = activate(space_forward(wide_space(v), wsv.at[j]))
+            hidden, slope = activate(space_forward(wide_space(v), wv.at[j]))
             bact[j] = slope
 
             @pl.when(j < 3)
             def _():
-                out = v + nn(wide_time(hidden), wtv[j])
+                out = v + nn(wide_time(hidden), wv[j, SPACE : SPACE + TIME, :])
                 bx[j + 1] = out.astype(BF16)
 
             return carry
@@ -346,8 +383,8 @@
             @pl.when(j + half > 0)
             def _():
                 g = bg[j + 1].astype(F32)
-                g_pre = (g_hidden_of(g, wtv.at[j]) * bact[j]).astype(BF16).astype(F32)
-                bg[j] = (g + space_backward(g_pre, wsv.at[j])).astype(BF16)
+                g_pre = (g_hidden_of(g, wv.at[j]) * bact[j]).astype(BF16).astype(F32)
+                bg[j] = (g + space_backward(g_pre, wv.at[j])).astype(BF16)
 
             return carry
 
@@ -378,7 +415,7 @@
 
         keep(gb, c, gin[c])
         g = gin[c].astype(F32)
-        keep(gp, c, (g_hidden_of(g, wtv.at[x]) * act[c]).astype(BF16))
+        keep(gp, c, (g_hidden_of(g, wv.at[x]) * act[c]).astype(BF16))
         return carry
 
     lax.fori_loop(0, 2, clip_back, 0)
@@ -484,13 +521,24 @@
         y_step(i).wait_send()
     for i in range(1, 8):
         z_step(i).wait_send()
-    for c in weight_copies(x, near, 0):
-        c.wait_send()
-
-    @pl.when(jnp.logical_not(end))
-    def _():
-        for c in weight_copies(x, 3 - near, 1):
-            c.wait_send()
+    @each
+    def _(c):
+        x_chunk(x, c, near, 0).wait_send()
+
+        @pl.when(middle)
+        def _():
+            x_chunk(x, c, 3 - x, 1).wait_send()
+
+        @pl.when(passes)
+        def _():
+            x_chunk(passed, c, near, 2).wait_send()
+
+        @pl.when(end)
+        def _():
+            for j in (passed, other, distant):
+                y_chunk(j, c, odd).wait_send()
+                core_chunk(j, c, 0, k).wait_send()
+                core_chunk(j, c, 1, k).wait_send()
 
     @pl.when(jnp.logical_or(S == 4, S == 7))
     def _():
@@ -505,11 +553,6 @@
     def _():
         for i in range(1, 4):
             j = lax.rem(x + i, 4)
-            for c in y_copies(j, 0, odd) + y_copies(j, 1, odd):
-                c.wait_send()
-            for n in range(3):
-                for c in share_copies(j, n, k):
-                    c.wait_send()
             g_copy(j).wait_send()
 
             @pl.when(half == 1)
@@ -534,8 +577,7 @@
         in_specs=[pl.BlockSpec(memory_space=pltpu.HBM)] * 4,
         out_specs=(pl.BlockSpec(memory_space=pltpu.VMEM),) * 2,
         scratch_shapes=[
-            vmem((4, SPACE, C), BF16),
-            vmem((4, TIME, C), BF16),
+            vmem((4, SPACE + TIME, C), BF16),
             vmem((2, ROWS, C), BF16),
             vmem((ROWS, C), BF16),
             vmem((2, ROWS, C), BF16),
@@ -558,12 +600,12 @@
             vmem((7, 96, 128), BF16),
             vmem((2, 96, 128), F32),
             sem((3,)),
-            sem((2, 2)),
-            sem((4, 2)),
-            sem((4, 3, 2)),
-            sem((4, 3, 2)),
-            sem((4, 2, 2)),
-            sem((4, 2, 2)),
+            sem((3, 4)),
+            sem((4, 4)),
+            sem((4, 8)),
+            sem((4, 8)),
+            sem((4, 4)),
+            sem((4, 4)),
             sem((2,)),
             sem((2,)),
             sem((4,)),

time: 88.8 us -> 83.9 us (0.945)
  Pallas kernels: 85.2 us -> 80.3 us
    pallas_call x1, Pallas kernels: 85.2 us -> 80.3 us  [body(): pl.pallas_call(functools.partial(kernel, scale), out_shape=(jax.ShapeDtyp...]
where the time goes in v4:
time: 83.9 us; the launch traced here: 83.7 us
  Pallas kernels  80.3 us (96%)
  local copies, waits for them, and re-layouts  2.76 us (3%)
    pallas_call x1, Pallas kernels, body(): pl.pallas_call(functools.partial(kernel, scale), out_shape=(jax.ShapeDtyp...  80.3 us
    unnamed x2, local copies, waits for them, and re-layouts  2.76 us

profile of v4, /device:TPU:1, one launch (start us, length us, event | category | flops | bytes accessed | tf_op | source)
XLA Modules:
  0.0 83.7 jit_solution(14995860644975757691)
XLA Ops:
  0.6 80.3 %window.1 = (f32[36,256]{1,0:T(8,128)}, f32[12,256]{1,0:T(8,128)}) custom-call(bf16[2,128,256]{2,1,0:T(8,128)(2,1)} %bitcast.8, bf16[2,128,256]{2,1,0:T(8,128)(2,1)} %bitcast.9, bf16[2304,256]{1,0:T(8,128)(2,1)} %bitcast.6, bf16[768,256]{1,0:T(8,128)(2,1)} %bitcast.7), custom_call_target="tpu_custom_call" | custom-call | tf_op jit(solution)/shard_map/window/pallas_call | solution.py:574
  80.9 1.4 %copy.6 = f32[1,36,256]{2,0,1:T(1,128)} copy(f32[1,36,256]{2,1,0:T(8,128)} %bitcast.10) | data formatting | bytes 73728
  82.3 1.3 %copy.7 = f32[1,12,256]{2,0,1:T(1,128)} copy(f32[1,12,256]{2,1,0:T(8,128)} %bitcast.11) | data formatting | bytes 24576

commit v5 on v4

--- a/solution.py
+++ b/solution.py
@@ -100,7 +100,7 @@
     loc, wg_send, wg_recv, ws_send, ws_recv, wy_send, wy_recv,
     x_send, x_recv, bx_send, bx_recv, ct_send, ct_recv,
     go_send, gin_recv, bg_send, bg_recv,
-    r1_send, r1_recv, r2_send, r2_recv, r3_send, r3_recv, r4_sem,
+    r1_send, r1_recv, r2_send, r2_recv, r3_send, r3_recv, r4_sem, up, down,
 ):
     S = lax.axis_index("section")
     D = lax.axis_index("dp")
@@ -141,11 +141,18 @@
         )
 
     hello(S, sibling)
-    for i in range(1, 4):
-        hello(S, lax.rem(y + i, 4) * 16 + lax.rem(D, 16))
-        hello(base + lax.rem(x + i, 4), D)
-    for i in range(1, 8):
-        hello(S, y * 16 + lax.rem(z + i, 8) * 2 + k)
+    hello(S, above)
+    hello(S, below)
+    hello(base + lax.rem(x + 1, 4), D)
+    hello(base + lax.rem(x + 3, 4), D)
+
+    @pl.when(z > 0)
+    def _():
+        hello(S, D - 2)
+
+    @pl.when(z < 7)
+    def _():
+        hello(S, D + 2)
 
     @pl.when(S == 0)
     def _():
@@ -153,20 +160,37 @@
 
     @pl.when(S == 3)
     def _():
-        hello(4, far)
         hello(7, far)
 
-    @pl.when(S == 4)
-    def _():
-        hello(0, far)
+    @pl.when(jnp.logical_or(S == 4, S == 7))
+    def _():
         hello(3, far)
 
-    @pl.when(S == 7)
-    def _():
-        hello(3, far)
-
-    crossings = jnp.where(end, 1, 0) + jnp.where(jnp.logical_or(S == 3, S == 4), 1, 0)
-    pl.semaphore_wait(barrier, 14 + crossings)
+    inner = jnp.logical_and(z > 0, z < 7)
+    crossings = jnp.where(S == 3, 2, jnp.where(jnp.logical_or(S == 4, S == 7), 1, 0))
+    pl.semaphore_wait(barrier, 6 + jnp.where(inner, 1, 0) + crossings)
+
+    def sweep(sem, step, first, last):
+        @pl.when(z != first)
+        def _():
+            pl.semaphore_wait(sem, 1)
+
+        @pl.when(z != last)
+        def _():
+            pl.semaphore_signal(
+                sem, inc=1, device_id={"section": S, "dp": D + 2 * step}, device_id_type=MESH
+            )
+
+    def meet_line():
+        @pl.when(z < 4)
+        def _():
+            sweep(up, 1, 0, 7)
+            sweep(down, -1, 7, 0)
+
+        @pl.when(z >= 4)
+        def _():
+            sweep(down, -1, 7, 0)
+            sweep(up, 1, 0, 7)
 
     for c in local:
         c.wait()
@@ -232,15 +256,21 @@
         def _():
             x_chunk(x, c, 3 - x, 1).start()
 
-    cot_copy = copy(cot_ref.at[mine], ct, ct_send, ct_recv, S, far)
-
-    @pl.when(jnp.logical_or(S == 4, S == 7))
-    def _():
-        cot_copy.start()
+    def cot_copy(c):
+        return copy(cot_ref.at[c], ct, ct_send.at[c], ct_recv, jnp.where(c == 0, 7, 4), far)
+
+    @pl.when(S == 3)
+    def _():
+        for c in range(2):
+            cot_copy(c).start()
 
     @pl.when(half == 1)
     def _():
         pass_middle()
+
+        @pl.when(jnp.logical_not(end))
+        def _():
+            meet_line()
 
     def rows_of(c, h):
         return pl.ds(pl.multiple_of(h * 128 + c * HALF, HALF), HALF)
@@ -304,6 +334,10 @@
         forward(False)
         pass_middle()
 
+        @pl.when(x < 3)
+        def _():
+            meet_line()
+
     def x_copy(j):
         return copy(bx.at[j], xin.at[mine], bx_send.at[j], x_recv.at[mine], base + j, D)
 
@@ -362,11 +396,12 @@
 
         @pl.when(half == 0)
         def _():
+            meet_line()
             back_copy.wait_recv()
 
         @pl.when(half == 1)
         def _():
-            cot_copy.wait_recv()
+            cot_copy(0).wait_recv()
             bg[4] = by_height(ct[...]).astype(BF16)
 
         def layer_back(i, carry):
@@ -393,6 +428,7 @@
         @pl.when(half == 1)
         def _():
             back_copy.start()
+            meet_line()
 
     @pl.when(half == 1)
     def _():
@@ -540,9 +576,10 @@
                 core_chunk(j, c, 0, k).wait_send()
                 core_chunk(j, c, 1, k).wait_send()
 
-    @pl.when(jnp.logical_or(S == 4, S == 7))
-    def _():
-        cot_copy.wait_send()
+    @pl.when(S == 3)
+    def _():
+        for c in range(2):
+            cot_copy(c).wait_send()
 
     @pl.when(half == 0)
     def _():
@@ -610,7 +647,7 @@
             sem((2,)),
             sem((4,)),
             sem,
-            sem,
+            sem((2,)),
             sem,
             sem((4,)),
             sem((2,)),
@@ -623,6 +660,8 @@
             sem((7,)),
             sem((7,)),
             sem((2,)),
+            pltpu.SemaphoreType.REGULAR,
+            pltpu.SemaphoreType.REGULAR,
         ],
         compiler_params=pltpu.CompilerParams(
             collective_id=0, has_side_effects=True, vmem_limit_bytes=66_900_000

time: 83.9 us -> 83.3 us (level)
  no operation moved by 1% of the time
where the time goes in v5:
time: 83.3 us; the launch traced here: 83 us
  Pallas kernels  79.6 us (96%)
  local copies, waits for them, and re-layouts  2.76 us (3%)
    pallas_call x1, Pallas kernels, body(): pl.pallas_call(functools.partial(kernel, scale), out_shape=(jax.ShapeDtyp...  79.6 us
    unnamed x2, local copies, waits for them, and re-layouts  2.76 us

profile of v5, /device:TPU:1, one launch (start us, length us, event | category | flops | bytes accessed | tf_op | source)
XLA Modules:
  0.0 83.0 jit_solution(13173958944664524275)
XLA Ops:
  0.6 79.6 %window.1 = (f32[36,256]{1,0:T(8,128)}, f32[12,256]{1,0:T(8,128)}) custom-call(bf16[2,128,256]{2,1,0:T(8,128)(2,1)} %bitcast.8, bf16[2,128,256]{2,1,0:T(8,128)(2,1)} %bitcast.9, bf16[2304,256]{1,0:T(8,128)(2,1)} %bitcast.6, bf16[768,256]{1,0:T(8,128)(2,1)} %bitcast.7), custom_call_target="tpu_custom_call" | custom-call | tf_op jit(solution)/shard_map/window/pallas_call | solution.py:611
  80.3 1.4 %copy.6 = f32[1,36,256]{2,0,1:T(1,128)} copy(f32[1,36,256]{2,1,0:T(8,128)} %bitcast.10) | data formatting | bytes 73728
  81.7 1.3 %copy.7 = f32[1,12,256]{2,0,1:T(1,128)} copy(f32[1,12,256]{2,1,0:T(8,128)} %bitcast.11) | data formatting | bytes 24576

commit v6 on v5

--- a/solution.py
+++ b/solution.py
@@ -165,9 +165,10 @@
     @pl.when(jnp.logical_or(S == 4, S == 7))
     def _():
         hello(3, far)
+        hello(S, far)
 
     inner = jnp.logical_and(z > 0, z < 7)
-    crossings = jnp.where(S == 3, 2, jnp.where(jnp.logical_or(S == 4, S == 7), 1, 0))
+    crossings = jnp.where(jnp.logical_or(S == 3, jnp.logical_or(S == 4, S == 7)), 2, 0)
     pl.semaphore_wait(barrier, 6 + jnp.where(inner, 1, 0) + crossings)
 
     def sweep(sem, step, first, last):
@@ -199,8 +200,7 @@
     passed = jnp.where(x % 2 == 0, 1, 2)
     other = jnp.where(x == 0, 3, 0)
     distant = jnp.where(x == 0, 2, 1)
-    middle = jnp.logical_and(jnp.logical_not(end), k == 1)
-    passes = jnp.logical_or(middle, jnp.logical_and(end, k == 0))
+    middle = jnp.logical_not(end)
 
     def chunk_copy(j, c, parity, core, send, recv, section, dp):
         n = 8 * parity + 4 * core + 2 * (c % 2) + c // 2
@@ -230,7 +230,7 @@
         x_chunk(j, c, 0, 0).wait_recv()
         y_chunk(j, c, odd).start()
 
-        @pl.when(jnp.logical_and(j == passed, k == 0))
+        @pl.when(jnp.logical_and(j == passed, c < 2))
         def _():
             x_chunk(j, c, near, 2).start()
 
@@ -243,8 +243,7 @@
     def pass_middle():
         @pl.when(middle)
         def _():
-            @each
-            def _(c):
+            for c in (2, 3):
                 x_chunk(passed, c, 0, 0).wait_recv()
                 x_chunk(passed, c, near, 2).start()
 
@@ -252,17 +251,15 @@
     def _(c):
         x_chunk(x, c, near, 0).start()
 
-        @pl.when(middle)
+        @pl.when(jnp.logical_and(middle, c >= 2))
         def _():
             x_chunk(x, c, 3 - x, 1).start()
 
-    def cot_copy(c):
-        return copy(cot_ref.at[c], ct, ct_send.at[c], ct_recv, jnp.where(c == 0, 7, 4), far)
-
-    @pl.when(S == 3)
-    def _():
-        for c in range(2):
-            cot_copy(c).start()
+    cot_copy = copy(cot_ref.at[mine], ct, ct_send, ct_recv, S, far)
+
+    @pl.when(jnp.logical_or(S == 4, S == 7))
+    def _():
+        cot_copy.start()
 
     @pl.when(half == 1)
     def _():
@@ -282,8 +279,9 @@
     def y_copy(c):
         return copy(yout.at[c], xin.at[c], x_send.at[c], x_recv.at[c], lax.rem(S + 1, 8), D)
 
-    def y_cross(c):
-        return copy(yout.at[c], bx.at[0], x_send.at[c], bx_recv, jnp.where(c == 0, 7, 4), far)
+    cross_copy = copy(yout.at[0], bx.at[0], x_send.at[0], bx_recv, 7, far)
+    hand_copy = copy(yout.at[1], ct, x_send.at[1], ct_recv, 0, D)
+    relay_copy = copy(ct, bx.at[0], ct_send, bx_recv, 4, far)
 
     def owner_hidden(c):
         wide = wide_space(xin[c].astype(F32))
@@ -310,9 +308,13 @@
                 def _():
                     y_copy(c).start()
 
-                @pl.when(x == 3)
+                @pl.when(jnp.logical_and(x == 3, c == 0))
                 def _():
-                    y_cross(c).start()
+                    cross_copy.start()
+
+                @pl.when(jnp.logical_and(x == 3, c == 1))
+                def _():
+                    hand_copy.start()
 
             return carry
 
@@ -328,6 +330,11 @@
         def _(c):
             take_x(passed, c)
             take_x(other, c)
+
+    @pl.when(S == 0)
+    def _():
+        hand_copy.wait_recv()
+        relay_copy.start()
 
     @pl.when(jnp.logical_and(half == 0, x > 0))
     def _():
@@ -368,7 +375,7 @@
 
         @pl.when(half == 1)
         def _():
-            y_cross(0).wait_recv()
+            cross_copy.wait_recv()
 
         def layer(j, carry):
             @pl.when(half == 1)
@@ -401,7 +408,7 @@
 
         @pl.when(half == 1)
         def _():
-            cot_copy(0).wait_recv()
+            cot_copy.wait_recv()
             bg[4] = by_height(ct[...]).astype(BF16)
 
         def layer_back(i, carry):
@@ -463,10 +470,8 @@
         dw[768 + 256 * q : 1024 + 256 * q, :] = tn(xc[:, lanes], gp[...])
         dw[1536 + 256 * q : 1792 + 256 * q, :] = tn(xc[128:256, lanes], gp[0:128, :])
 
-    ahead = jnp.where(odd == k, 1, 3)
     blocks = [lax.rem(y + i, 4) for i in (2, 1, 3, 0)]
-    forth = lax.rem(y + ahead, 4)
-    back = lax.rem(y + 4 - ahead, 4)
+    sides = (lax.rem(y + 1, 4), lax.rem(y + 3, 4))
 
     def core_step(i, column):
         yb = blocks[i]
@@ -485,38 +490,45 @@
         lax.fori_loop(0, 8, pack, 0)
         core_step(i, 1 - k).start()
 
-    def add_cores(yb):
+    def add_cores(yb, start, stop):
         def one(b, carry):
             s1[yb, b] = (part[k, yb, b].astype(F32) + r1[yb, b].astype(F32)).astype(BF16)
             return carry
 
-        lax.fori_loop(0, 8, one, 0)
-
-    def y_step(i):
+        lax.fori_loop(start, stop, one, 0)
+
+    def y_step(i, side):
+        forth, back = sides[side], sides[1 - side]
+        to = (forth, back, forth)[i]
+        some = pl.ds(4 * side, 4)
         return copy(
-            s1.at[(blocks[0], forth, back)[i]], r2.at[i], r2_send.at[i], r2_recv.at[i],
-            S, (forth, forth, back)[i] * 16 + lane,
+            s1.at[blocks[0] if i == 0 else to, some], r2.at[i, some],
+            r2_send.at[i, side], r2_recv.at[i, side], S, to * 16 + lane,
         )
 
     core_step(0, k).wait_recv()
-    add_cores(blocks[0])
-    y_step(0).start()
-    core_step(1, k).wait_recv()
-    core_step(2, k).wait_recv()
-    add_cores(forth)
-    y_step(1).start()
-    y_step(0).wait_recv()
-
-    def add_relayed(b, carry):
-        total = part[k, back, b].astype(F32) + r1[back, b].astype(F32) + r2[0, b].astype(F32)
-        s1[back, b] = total.astype(BF16)
-        return carry
-
-    lax.fori_loop(0, 8, add_relayed, 0)
-    y_step(2).start()
+    add_cores(blocks[0], 0, 8)
+    y_step(0, 0).start()
+    y_step(0, 1).start()
+    for side in (1, 0):
+        core_step(2 - side, k).wait_recv()
+        add_cores(sides[1 - side], 4 * side, 4 * side + 4)
+        y_step(1, side).start()
+    for side in range(2):
+        forth = sides[side]
+        y_step(0, side).wait_recv()
+
+        def add_relayed(b, carry):
+            total = part[k, forth, b].astype(F32) + r1[forth, b].astype(F32) + r2[0, b].astype(F32)
+            s1[forth, b] = total.astype(BF16)
+            return carry
+
+        lax.fori_loop(4 * side, 4 * side + 4, add_relayed, 0)
+        y_step(2, side).start()
     core_step(3, k).wait_recv()
-    y_step(1).wait_recv()
-    y_step(2).wait_recv()
+    for i in (1, 2):
+        for side in range(2):
+            y_step(i, side).wait_recv()
     def add_y(b, carry):
         total = part[k, y, b].astype(F32) + r1[y, b].astype(F32) + r2[1, b].astype(F32) + r2[2, b].astype(F32)
         s2[b] = total.astype(BF16)
@@ -554,18 +566,19 @@
     for i in range(4):
         core_step(i, 1 - k).wait_send()
     for i in range(3):
-        y_step(i).wait_send()
+        for side in range(2):
+            y_step(i, side).wait_send()
     for i in range(1, 8):
         z_step(i).wait_send()
     @each
     def _(c):
         x_chunk(x, c, near, 0).wait_send()
 
-        @pl.when(middle)
+        @pl.when(jnp.logical_and(middle, c >= 2))
         def _():
             x_chunk(x, c, 3 - x, 1).wait_send()
 
-        @pl.when(passes)
+        @pl.when(middle == (c >= 2))
         def _():
             x_chunk(passed, c, near, 2).wait_send()
 
@@ -576,10 +589,13 @@
                 core_chunk(j, c, 0, k).wait_send()
                 core_chunk(j, c, 1, k).wait_send()
 
-    @pl.when(S == 3)
-    def _():
-        for c in range(2):
-            cot_copy(c).wait_send()
+    @pl.when(jnp.logical_or(S == 4, S == 7))
+    def _():
+        cot_copy.wait_send()
+
+    @pl.when(S == 0)
+    def _():
+        relay_copy.wait_send()
 
     @pl.when(half == 0)
     def _():
@@ -647,7 +663,7 @@
             sem((2,)),
             sem((4,)),
             sem,
-            sem((2,)),
+            sem,
             sem,
             sem((4,)),
             sem((2,)),
@@ -655,8 +671,8 @@
             sem,
             sem((4,)),
             sem((4,)),
-            sem((3,)),
-            sem((3,)),
+            sem((3, 2)),
+            sem((3, 2)),
             sem((7,)),
             sem((7,)),
             sem((2,)),

time: 83.3 us -> 82.2 us (0.987)
  Pallas kernels: 79.6 us -> 78.6 us
    pallas_call x1, Pallas kernels: 79.6 us -> 78.6 us  [body(): pl.pallas_call(functools.partial(kernel, scale), out_shape=(jax.ShapeDtyp...]
where the time goes in v6:
time: 82.2 us; the launch traced here: 82 us
  Pallas kernels  78.6 us (96%)
  local copies, waits for them, and re-layouts  2.76 us (3%)
    pallas_call x1, Pallas kernels, body(): pl.pallas_call(functools.partial(kernel, scale), out_shape=(jax.ShapeDtyp...  78.6 us
    unnamed x2, local copies, waits for them, and re-layouts  2.76 us

profile of v6, /device:TPU:1, one launch (start us, length us, event | category | flops | bytes accessed | tf_op | source)
XLA Modules:
  0.0 82.0 jit_solution(13629435638568947029)
XLA Ops:
  0.6 78.6 %window.1 = (f32[36,256]{1,0:T(8,128)}, f32[12,256]{1,0:T(8,128)}) custom-call(bf16[2,128,256]{2,1,0:T(8,128)(2,1)} %bitcast.8, bf16[2,128,256]{2,1,0:T(8,128)(2,1)} %bitcast.9, bf16[2304,256]{1,0:T(8,128)(2,1)} %bitcast.6, bf16[768,256]{1,0:T(8,128)(2,1)} %bitcast.7), custom_call_target="tpu_custom_call" | custom-call | tf_op jit(solution)/shard_map/window/pallas_call | solution.py:627
  79.2 1.4 %copy.6 = f32[1,36,256]{2,0,1:T(1,128)} copy(f32[1,36,256]{2,1,0:T(8,128)} %bitcast.10) | data formatting | bytes 73728
  80.7 1.3 %copy.7 = f32[1,12,256]{2,0,1:T(1,128)} copy(f32[1,12,256]{2,1,0:T(8,128)} %bitcast.11) | data formatting | bytes 24576

commit v7 on v6

--- a/solution.py
+++ b/solution.py
@@ -100,7 +100,7 @@
     loc, wg_send, wg_recv, ws_send, ws_recv, wy_send, wy_recv,
     x_send, x_recv, bx_send, bx_recv, ct_send, ct_recv,
     go_send, gin_recv, bg_send, bg_recv,
-    r1_send, r1_recv, r2_send, r2_recv, r3_send, r3_recv, r4_sem, up, down,
+    r1_send, r1_recv, r2_send, r2_recv, r3_send, r3_recv, r4_sem, up, down, answer,
 ):
     S = lax.axis_index("section")
     D = lax.axis_index("dp")
@@ -164,12 +164,17 @@
 
     @pl.when(jnp.logical_or(S == 4, S == 7))
     def _():
-        hello(3, far)
         hello(S, far)
 
     inner = jnp.logical_and(z > 0, z < 7)
-    crossings = jnp.where(jnp.logical_or(S == 3, jnp.logical_or(S == 4, S == 7)), 2, 0)
+    crossings = jnp.where(jnp.logical_or(S == 4, S == 7), 2, 0)
     pl.semaphore_wait(barrier, 6 + jnp.where(inner, 1, 0) + crossings)
+
+    @pl.when(jnp.logical_or(S == 4, S == 7))
+    def _():
+        pl.semaphore_signal(
+            answer, inc=1, device_id={"section": lax.rem(S + 4, 8), "dp": far}, device_id_type=MESH
+        )
 
     def sweep(sem, step, first, last):
         @pl.when(z != first)
@@ -230,9 +235,10 @@
         x_chunk(j, c, 0, 0).wait_recv()
         y_chunk(j, c, odd).start()
 
-        @pl.when(jnp.logical_and(j == passed, c < 2))
-        def _():
-            x_chunk(j, c, near, 2).start()
+        if c in (0, 3):
+            @pl.when(j == passed)
+            def _():
+                x_chunk(j, c, near, 2).start()
 
         core_chunk(j, c, 0, k).start()
 
@@ -243,16 +249,17 @@
     def pass_middle():
         @pl.when(middle)
         def _():
-            for c in (2, 3):
+            for c in (1, 2):
                 x_chunk(passed, c, 0, 0).wait_recv()
                 x_chunk(passed, c, near, 2).start()
-
-    @each
-    def _(c):
+                x_chunk(x, c + 1, near, 0).start()
+
+    for c in (0, 1):
         x_chunk(x, c, near, 0).start()
 
-        @pl.when(jnp.logical_and(middle, c >= 2))
-        def _():
+    @pl.when(middle)
+    def _():
+        for c in (1, 2):
             x_chunk(x, c, 3 - x, 1).start()
 
     cot_copy = copy(cot_ref.at[mine], ct, ct_send, ct_recv, S, far)
@@ -310,6 +317,7 @@
 
                 @pl.when(jnp.logical_and(x == 3, c == 0))
                 def _():
+                    pl.semaphore_wait(answer, 1)
                     cross_copy.start()
 
                 @pl.when(jnp.logical_and(x == 3, c == 1))
@@ -326,14 +334,15 @@
 
     @pl.when(end)
     def _():
-        @each
-        def _(c):
+        for c in (0, 1):
             take_x(passed, c)
             take_x(other, c)
+            x_chunk(x, c + 2, near, 0).start()
 
     @pl.when(S == 0)
     def _():
         hand_copy.wait_recv()
+        pl.semaphore_wait(answer, 1)
         relay_copy.start()
 
     @pl.when(jnp.logical_and(half == 0, x > 0))
@@ -355,14 +364,23 @@
 
     @pl.when(end)
     def _():
-        @each
-        def _(c):
-            take_x(distant, c)
-            take_y(passed, c)
-            take_y(other, c)
-        @each
-        def _(c):
-            take_y(distant, c)
+        def take_ys(*pairs):
+            for j, c in pairs:
+                take_y(j, c)
+
+        take_x(distant, 0)
+        take_x(distant, 1)
+        take_ys((passed, 0), (other, 0))
+        take_x(passed, 2)
+        take_x(other, 2)
+        take_ys((passed, 1), (other, 1))
+        take_x(distant, 2)
+        take_ys((distant, 0), (distant, 1))
+        take_x(passed, 3)
+        take_x(other, 3)
+        take_ys((passed, 2), (other, 2))
+        take_x(distant, 3)
+        take_ys((distant, 2), (passed, 3), (other, 3), (distant, 3))
         @each
         def _(c):
             for j in (passed, other, distant):
@@ -574,11 +592,13 @@
     def _(c):
         x_chunk(x, c, near, 0).wait_send()
 
-        @pl.when(jnp.logical_and(middle, c >= 2))
+        between = jnp.logical_or(c == 1, c == 2)
+
+        @pl.when(jnp.logical_and(middle, between))
         def _():
             x_chunk(x, c, 3 - x, 1).wait_send()
 
-        @pl.when(middle == (c >= 2))
+        @pl.when(middle == between)
         def _():
             x_chunk(passed, c, near, 2).wait_send()
 
@@ -678,6 +698,7 @@
             sem((2,)),
             pltpu.SemaphoreType.REGULAR,
             pltpu.SemaphoreType.REGULAR,
+            pltpu.SemaphoreType.REGULAR,
         ],
         compiler_params=pltpu.CompilerParams(
             collective_id=0, has_side_effects=True, vmem_limit_bytes=66_900_000

time: 82.2 us -> 85.4 us (1.039)
  Pallas kernels: 78.6 us -> 81.7 us
    pallas_call x1, Pallas kernels: 78.6 us -> 81.7 us  [body(): pl.pallas_call(functools.partial(kernel, scale), out_shape=(jax.ShapeDtyp...]
where the time goes in v7:
time: 85.4 us; the launch traced here: 85.1 us
  Pallas kernels  81.7 us (96%)
  local copies, waits for them, and re-layouts  2.76 us (3%)
    pallas_call x1, Pallas kernels, body(): pl.pallas_call(functools.partial(kernel, scale), out_shape=(jax.ShapeDtyp...  81.7 us
    unnamed x2, local copies, waits for them, and re-layouts  2.76 us

profile of v7, /device:TPU:1, one launch (start us, length us, event | category | flops | bytes accessed | tf_op | source)
XLA Modules:
  0.0 85.1 jit_solution(2684295347658190354)
XLA Ops:
  0.6 81.7 %window.1 = (f32[36,256]{1,0:T(8,128)}, f32[12,256]{1,0:T(8,128)}) custom-call(bf16[2,128,256]{2,1,0:T(8,128)(2,1)} %bitcast.8, bf16[2,128,256]{2,1,0:T(8,128)(2,1)} %bitcast.9, bf16[2304,256]{1,0:T(8,128)(2,1)} %bitcast.6, bf16[768,256]{1,0:T(8,128)(2,1)} %bitcast.7), custom_call_target="tpu_custom_call" | custom-call | tf_op jit(solution)/shard_map/window/pallas_call | solution.py:647
  82.3 1.4 %copy.6 = f32[1,36,256]{2,0,1:T(1,128)} copy(f32[1,36,256]{2,1,0:T(8,128)} %bitcast.10) | data formatting | bytes 73728
  83.8 1.3 %copy.7 = f32[1,12,256]{2,0,1:T(1,128)} copy(f32[1,12,256]{2,1,0:T(8,128)} %bitcast.11) | data formatting | bytes 24576

commit v8 on v6

--- a/solution.py
+++ b/solution.py
@@ -100,7 +100,7 @@
     loc, wg_send, wg_recv, ws_send, ws_recv, wy_send, wy_recv,
     x_send, x_recv, bx_send, bx_recv, ct_send, ct_recv,
     go_send, gin_recv, bg_send, bg_recv,
-    r1_send, r1_recv, r2_send, r2_recv, r3_send, r3_recv, r4_sem, up, down,
+    r1_send, r1_recv, r2_send, r2_recv, r3_send, r3_recv, r4_sem, up, down, answer,
 ):
     S = lax.axis_index("section")
     D = lax.axis_index("dp")
@@ -164,12 +164,17 @@
 
     @pl.when(jnp.logical_or(S == 4, S == 7))
     def _():
-        hello(3, far)
         hello(S, far)
 
     inner = jnp.logical_and(z > 0, z < 7)
-    crossings = jnp.where(jnp.logical_or(S == 3, jnp.logical_or(S == 4, S == 7)), 2, 0)
+    crossings = jnp.where(jnp.logical_or(S == 4, S == 7), 2, 0)
     pl.semaphore_wait(barrier, 6 + jnp.where(inner, 1, 0) + crossings)
+
+    @pl.when(jnp.logical_or(S == 4, S == 7))
+    def _():
+        pl.semaphore_signal(
+            answer, inc=1, device_id={"section": lax.rem(S + 4, 8), "dp": far}, device_id_type=MESH
+        )
 
     def sweep(sem, step, first, last):
         @pl.when(z != first)
@@ -202,6 +207,9 @@
     distant = jnp.where(x == 0, 2, 1)
     middle = jnp.logical_not(end)
 
+    def between(c):
+        return jnp.logical_or(c == 1, c == 2)
+
     def chunk_copy(j, c, parity, core, send, recv, section, dp):
         n = 8 * parity + 4 * core + 2 * (c % 2) + c // 2
         rows = pl.ds(pl.multiple_of(n * 192, 192), 192)
@@ -230,7 +238,7 @@
         x_chunk(j, c, 0, 0).wait_recv()
         y_chunk(j, c, odd).start()
 
-        @pl.when(jnp.logical_and(j == passed, c < 2))
+        @pl.when(jnp.logical_and(j == passed, jnp.logical_not(between(c))))
         def _():
             x_chunk(j, c, near, 2).start()
 
@@ -243,7 +251,7 @@
     def pass_middle():
         @pl.when(middle)
         def _():
-            for c in (2, 3):
+            for c in (1, 2):
                 x_chunk(passed, c, 0, 0).wait_recv()
                 x_chunk(passed, c, near, 2).start()
 
@@ -251,7 +259,7 @@
     def _(c):
         x_chunk(x, c, near, 0).start()
 
-        @pl.when(jnp.logical_and(middle, c >= 2))
+        @pl.when(jnp.logical_and(middle, between(c)))
         def _():
             x_chunk(x, c, 3 - x, 1).start()
 
@@ -310,6 +318,7 @@
 
                 @pl.when(jnp.logical_and(x == 3, c == 0))
                 def _():
+                    pl.semaphore_wait(answer, 1)
                     cross_copy.start()
 
                 @pl.when(jnp.logical_and(x == 3, c == 1))
@@ -323,6 +332,10 @@
     @pl.when(S == 0)
     def _():
         forward(True)
+
+    @pl.when(jnp.logical_or(S == 0, S == 3))
+    def _():
+        meet_line()
 
     @pl.when(end)
     def _():
@@ -334,6 +347,7 @@
     @pl.when(S == 0)
     def _():
         hand_copy.wait_recv()
+        pl.semaphore_wait(answer, 1)
         relay_copy.start()
 
     @pl.when(jnp.logical_and(half == 0, x > 0))
@@ -403,7 +417,6 @@
 
         @pl.when(half == 0)
         def _():
-            meet_line()
             back_copy.wait_recv()
 
         @pl.when(half == 1)
@@ -574,11 +587,11 @@
     def _(c):
         x_chunk(x, c, near, 0).wait_send()
 
-        @pl.when(jnp.logical_and(middle, c >= 2))
+        @pl.when(jnp.logical_and(middle, between(c)))
         def _():
             x_chunk(x, c, 3 - x, 1).wait_send()
 
-        @pl.when(middle == (c >= 2))
+        @pl.when(middle == between(c))
         def _():
             x_chunk(passed, c, near, 2).wait_send()
 
@@ -678,6 +691,7 @@
             sem((2,)),
             pltpu.SemaphoreType.REGULAR,
             pltpu.SemaphoreType.REGULAR,
+            pltpu.SemaphoreType.REGULAR,
         ],
         compiler_params=pltpu.CompilerParams(
             collective_id=0, has_side_effects=True, vmem_limit_bytes=66_900_000

time: 82.2 us -> 81.7 us (level)
  no operation moved by 1% of the time
where the time goes in v8:
time: 81.7 us; the launch traced here: 81.4 us
  Pallas kernels  78 us (95%)
  local copies, waits for them, and re-layouts  2.76 us (3%)
    pallas_call x1, Pallas kernels, body(): pl.pallas_call(functools.partial(kernel, scale), out_shape=(jax.ShapeDtyp...  78 us
    unnamed x2, local copies, waits for them, and re-layouts  2.76 us

profile of v8, /device:TPU:1, one launch (start us, length us, event | category | flops | bytes accessed | tf_op | source)
XLA Modules:
  0.0 81.4 jit_solution(1167923486558383665)
XLA Ops:
  0.6 78.0 %window.1 = (f32[36,256]{1,0:T(8,128)}, f32[12,256]{1,0:T(8,128)}) custom-call(bf16[2,128,256]{2,1,0:T(8,128)(2,1)} %bitcast.8, bf16[2,128,256]{2,1,0:T(8,128)(2,1)} %bitcast.9, bf16[2304,256]{1,0:T(8,128)(2,1)} %bitcast.6, bf16[768,256]{1,0:T(8,128)(2,1)} %bitcast.7), custom_call_target="tpu_custom_call" | custom-call | tf_op jit(solution)/shard_map/window/pallas_call | solution.py:640
  78.6 1.4 %copy.6 = f32[1,36,256]{2,0,1:T(1,128)} copy(f32[1,36,256]{2,1,0:T(8,128)} %bitcast.10) | data formatting | bytes 73728
  80.1 1.3 %copy.7 = f32[1,12,256]{2,0,1:T(1,128)} copy(f32[1,12,256]{2,1,0:T(8,128)} %bitcast.11) | data formatting | bytes 24576

commit v9 on v8

--- a/solution.py
+++ b/solution.py
@@ -91,11 +91,26 @@
     return same + jnp.concatenate([top, bottom], axis=0)
 
 
+def g_hidden_turned(g, w):
+    before, after = frames(g)
+    wide = jnp.concatenate([after, g, before], axis=1).astype(BF16)
+    return nn(wide, w[SPACE : SPACE + TIME, :])
+
+
+def space_backward_turned(g_pre, w):
+    before, after = columns(g_pre)
+    wide = jnp.concatenate([after, g_pre, before], axis=1).astype(BF16)
+    same = nn(wide, w[768:1536, :])
+    top = nn(wide[HALF:], w[0:768, :])
+    bottom = nn(wide[:HALF], w[1536:2304, :])
+    return same + jnp.concatenate([top, bottom], axis=0)
+
+
 def kernel(
     scale,
     clips_ref, cot_ref, ws_ref, wt_ref,
     out_s, out_t,
-    wv, cl, ct, xin, yout, bx, bg, gin,
+    wv, turned, cl, ct, xin, yout, bx, bg, gin,
     act, bact, xc, hc, gp, gb, dw, part, r1, s1, r2, s2, r3, fin,
     loc, wg_send, wg_recv, ws_send, ws_recv, wy_send, wy_recv,
     x_send, x_recv, bx_send, bx_recv, ct_send, ct_recv,
@@ -162,12 +177,8 @@
     def _():
         hello(7, far)
 
-    @pl.when(jnp.logical_or(S == 4, S == 7))
-    def _():
-        hello(S, far)
-
     inner = jnp.logical_and(z > 0, z < 7)
-    crossings = jnp.where(jnp.logical_or(S == 4, S == 7), 2, 0)
+    crossings = jnp.where(jnp.logical_or(S == 4, S == 7), 1, 0)
     pl.semaphore_wait(barrier, 6 + jnp.where(inner, 1, 0) + crossings)
 
     @pl.when(jnp.logical_or(S == 4, S == 7))
@@ -263,11 +274,9 @@
         def _():
             x_chunk(x, c, 3 - x, 1).start()
 
-    cot_copy = copy(cot_ref.at[mine], ct, ct_send, ct_recv, S, far)
-
-    @pl.when(jnp.logical_or(S == 4, S == 7))
-    def _():
-        cot_copy.start()
+    cot_copy = copy(
+        cot_ref.at[jnp.where(x == 1, 1, 0)], ct, ct_send, ct_recv, jnp.where(x == 1, 4, 7), far
+    )
 
     @pl.when(half == 1)
     def _():
@@ -276,6 +285,7 @@
         @pl.when(jnp.logical_not(end))
         def _():
             meet_line()
+            cot_copy.start()
 
     def rows_of(c, h):
         return pl.ds(pl.multiple_of(h * 128 + c * HALF, HALF), HALF)
@@ -417,6 +427,12 @@
 
         @pl.when(half == 0)
         def _():
+            def turn(n, carry):
+                rows = pl.ds(pl.multiple_of((n % 12) * C, C), C)
+                turned[n // 12, rows] = wv[n // 12, rows].T
+                return carry
+
+            lax.fori_loop(12, 48, turn, 0)
             back_copy.wait_recv()
 
         @pl.when(half == 1)
@@ -424,26 +440,35 @@
             cot_copy.wait_recv()
             bg[4] = by_height(ct[...]).astype(BF16)
 
-        def layer_back(i, carry):
-            j = 3 - i
-
-            @pl.when(j == x)
-            def _():
-                gin[mine] = bg[j + 1]
-
-            @pl.when(j != x)
-            def _():
-                g_copy(j).start()
-
-            @pl.when(j + half > 0)
-            def _():
-                g = bg[j + 1].astype(F32)
-                g_pre = (g_hidden_of(g, wv.at[j]) * bact[j]).astype(BF16).astype(F32)
-                bg[j] = (g + space_backward(g_pre, wv.at[j])).astype(BF16)
-
-            return carry
-
-        lax.fori_loop(0, 4, layer_back, 0)
+        def layers_back(w, g_hidden, g_space):
+            def layer_back(i, carry):
+                j = 3 - i
+
+                @pl.when(j == x)
+                def _():
+                    gin[mine] = bg[j + 1]
+
+                @pl.when(j != x)
+                def _():
+                    g_copy(j).start()
+
+                @pl.when(j + half > 0)
+                def _():
+                    g = bg[j + 1].astype(F32)
+                    g_pre = (g_hidden(g, w.at[j]) * bact[j]).astype(BF16).astype(F32)
+                    bg[j] = (g + g_space(g_pre, w.at[j])).astype(BF16)
+
+                return carry
+
+            lax.fori_loop(0, 4, layer_back, 0)
+
+        @pl.when(half == 0)
+        def _():
+            layers_back(turned, g_hidden_turned, space_backward_turned)
+
+        @pl.when(half == 1)
+        def _():
+            layers_back(wv, g_hidden_of, space_backward)
 
         @pl.when(half == 1)
         def _():
@@ -602,7 +627,7 @@
                 core_chunk(j, c, 0, k).wait_send()
                 core_chunk(j, c, 1, k).wait_send()
 
-    @pl.when(jnp.logical_or(S == 4, S == 7))
+    @pl.when(jnp.logical_or(S == 5, S == 6))
     def _():
         cot_copy.wait_send()
 
@@ -643,6 +668,7 @@
         in_specs=[pl.BlockSpec(memory_space=pltpu.HBM)] * 4,
         out_specs=(pl.BlockSpec(memory_space=pltpu.VMEM),) * 2,
         scratch_shapes=[
+            vmem((4, SPACE + TIME, C), BF16),
             vmem((4, SPACE + TIME, C), BF16),
             vmem((2, ROWS, C), BF16),
             vmem((ROWS, C), BF16),

time: 81.7 us -> 80.9 us (level)
  Pallas kernels: 78 us -> 77.1 us
    pallas_call x1, Pallas kernels: 78 us -> 77.1 us  [body(): pl.pallas_call(functools.partial(kernel, scale), out_shape=(jax.ShapeDtyp...]
where the time goes in v9:
time: 80.9 us; the launch traced here: 80.5 us
  Pallas kernels  77.1 us (95%)
  local copies, waits for them, and re-layouts  2.76 us (3%)
    pallas_call x1, Pallas kernels, body(): pl.pallas_call(functools.partial(kernel, scale), out_shape=(jax.ShapeDtyp...  77.1 us
    unnamed x2, local copies, waits for them, and re-layouts  2.76 us

profile of v9, /device:TPU:1, one launch (start us, length us, event | category | flops | bytes accessed | tf_op | source)
XLA Modules:
  0.0 80.5 jit_solution(2897639422576062654)
XLA Ops:
  0.6 77.1 %window.1 = (f32[36,256]{1,0:T(8,128)}, f32[12,256]{1,0:T(8,128)}) custom-call(bf16[2,128,256]{2,1,0:T(8,128)(2,1)} %bitcast.8, bf16[2,128,256]{2,1,0:T(8,128)(2,1)} %bitcast.9, bf16[2304,256]{1,0:T(8,128)(2,1)} %bitcast.6, bf16[768,256]{1,0:T(8,128)(2,1)} %bitcast.7), custom_call_target="tpu_custom_call" | custom-call | tf_op jit(solution)/shard_map/window/pallas_call | solution.py:665
  77.8 1.4 %copy.6 = f32[1,36,256]{2,0,1:T(1,128)} copy(f32[1,36,256]{2,1,0:T(8,128)} %bitcast.10) | data formatting | bytes 73728
  79.2 1.3 %copy.7 = f32[1,12,256]{2,0,1:T(1,128)} copy(f32[1,12,256]{2,1,0:T(8,128)} %bitcast.11) | data formatting | bytes 24576

commit v10 on v9

--- a/solution.py
+++ b/solution.py
@@ -124,7 +124,7 @@
     y = D // 16
     z = (D // 2) % 8
     k = D % 2
-    far = D + 8 - 16 * (z // 4)
+    far = D + 14 - 4 * z
     sibling = D + 1 - 2 * k
     end = jnp.logical_or(x == 0, x == 3)
     mine = jnp.where(x == 0, 1, 0)
@@ -278,9 +278,18 @@
         cot_ref.at[jnp.where(x == 1, 1, 0)], ct, ct_send, ct_recv, jnp.where(x == 1, 4, 7), far
     )
 
+    def turn(j, n):
+        rows = pl.ds(pl.multiple_of(n * C, C), C)
+        turned[j, rows] = wv[j, rows].T
+        return 0
+
     @pl.when(half == 1)
     def _():
         pass_middle()
+
+        @pl.when(end)
+        def _():
+            lax.fori_loop(0, 12, lambda n, carry: turn(x, n), 0)
 
         @pl.when(jnp.logical_not(end))
         def _():
@@ -427,12 +436,7 @@
 
         @pl.when(half == 0)
         def _():
-            def turn(n, carry):
-                rows = pl.ds(pl.multiple_of((n % 12) * C, C), C)
-                turned[n // 12, rows] = wv[n // 12, rows].T
-                return carry
-
-            lax.fori_loop(12, 48, turn, 0)
+            lax.fori_loop(12, 48, lambda n, carry: turn(n // 12, n % 12), 0)
             back_copy.wait_recv()
 
         @pl.when(half == 1)
@@ -440,35 +444,38 @@
             cot_copy.wait_recv()
             bg[4] = by_height(ct[...]).astype(BF16)
 
-        def layers_back(w, g_hidden, g_space):
-            def layer_back(i, carry):
+        def hand_out(j):
+            @pl.when(j == x)
+            def _():
+                gin[mine] = bg[j + 1]
+
+            @pl.when(j != x)
+            def _():
+                g_copy(j).start()
+
+        def layer_back(j, w, g_hidden, g_space):
+            g = bg[j + 1].astype(F32)
+            g_pre = (g_hidden(g, w.at[j]) * bact[j]).astype(BF16).astype(F32)
+            bg[j] = (g + g_space(g_pre, w.at[j])).astype(BF16)
+
+        def layers_back(is_turned, lowest):
+            def step(i, carry):
                 j = 3 - i
-
-                @pl.when(j == x)
+                hand_out(j)
+
+                @pl.when(jnp.logical_and(j >= lowest, is_turned(j)))
                 def _():
-                    gin[mine] = bg[j + 1]
-
-                @pl.when(j != x)
+                    layer_back(j, turned, g_hidden_turned, space_backward_turned)
+
+                @pl.when(jnp.logical_and(j >= lowest, jnp.logical_not(is_turned(j))))
                 def _():
-                    g_copy(j).start()
-
-                @pl.when(j + half > 0)
-                def _():
-                    g = bg[j + 1].astype(F32)
-                    g_pre = (g_hidden(g, w.at[j]) * bact[j]).astype(BF16).astype(F32)
-                    bg[j] = (g + g_space(g_pre, w.at[j])).astype(BF16)
+                    layer_back(j, wv, g_hidden_of, space_backward)
 
                 return carry
 
-            lax.fori_loop(0, 4, layer_back, 0)
-
-        @pl.when(half == 0)
-        def _():
-            layers_back(turned, g_hidden_turned, space_backward_turned)
-
-        @pl.when(half == 1)
-        def _():
-            layers_back(wv, g_hidden_of, space_backward)
+            lax.fori_loop(0, 4, step, 0)
+
+        layers_back(lambda j: jnp.logical_or(half == 0, j == x), 1 - half)
 
         @pl.when(half == 1)
         def _():
@@ -528,60 +535,82 @@
         lax.fori_loop(0, 8, pack, 0)
         core_step(i, 1 - k).start()
 
-    def add_cores(yb, start, stop):
+    def part_rows(r):
+        return slice(48 * r, 48 * r + 48)
+
+    def add_cores(yb, start, stop, rows):
         def one(b, carry):
-            s1[yb, b] = (part[k, yb, b].astype(F32) + r1[yb, b].astype(F32)).astype(BF16)
+            s1[yb, b, rows] = (part[k, yb, b, rows].astype(F32) + r1[yb, b, rows].astype(F32)).astype(BF16)
             return carry
 
         lax.fori_loop(start, stop, one, 0)
 
-    def y_step(i, side):
+    def y_step(i, side, r):
         forth, back = sides[side], sides[1 - side]
         to = (forth, back, forth)[i]
-        some = pl.ds(4 * side, 4)
+        some, rows = pl.ds(4 * side, 4), pl.ds(48 * r, 48)
         return copy(
-            s1.at[blocks[0] if i == 0 else to, some], r2.at[i, some],
-            r2_send.at[i, side], r2_recv.at[i, side], S, to * 16 + lane,
+            s1.at[blocks[0] if i == 0 else to, some, rows], r2.at[i, some, rows],
+            r2_send.at[i, side, r], r2_recv.at[i, side, r], S, to * 16 + lane,
         )
 
+    def z_step(i, r):
+        to = lax.rem(z + i, 8)
+        rows = pl.ds(48 * r, 48)
+        return copy(
+            s2.at[to, rows], r3.at[i - 1, rows], r3_send.at[i - 1, r], r3_recv.at[i - 1, r],
+            S, y * 16 + to * 2 + k,
+        )
+
     core_step(0, k).wait_recv()
-    add_cores(blocks[0], 0, 8)
-    y_step(0, 0).start()
-    y_step(0, 1).start()
+    for r in range(2):
+        add_cores(blocks[0], 0, 8, part_rows(r))
+        for side in range(2):
+            y_step(0, side, r).start()
     for side in (1, 0):
         core_step(2 - side, k).wait_recv()
-        add_cores(sides[1 - side], 4 * side, 4 * side + 4)
-        y_step(1, side).start()
+        add_cores(sides[1 - side], 4 * side, 4 * side + 4, slice(0, 96))
+        y_step(1, side, 0).start()
+    for r in range(2):
+        for side in range(2):
+            forth, rows = sides[side], part_rows(r)
+            y_step(0, side, r).wait_recv()
+
+            def add_relayed(b, carry):
+                total = part[k, forth, b, rows].astype(F32) + r1[forth, b, rows].astype(F32)
+                s1[forth, b, rows] = (total + r2[0, b, rows].astype(F32)).astype(BF16)
+                return carry
+
+            lax.fori_loop(4 * side, 4 * side + 4, add_relayed, 0)
+            y_step(2, side, r).start()
     for side in range(2):
-        forth = sides[side]
-        y_step(0, side).wait_recv()
-
-        def add_relayed(b, carry):
-            total = part[k, forth, b].astype(F32) + r1[forth, b].astype(F32) + r2[0, b].astype(F32)
-            s1[forth, b] = total.astype(BF16)
+        y_step(1, side, 1).start()
+    core_step(3, k).wait_recv()
+    for r in range(2):
+        rows = part_rows(r)
+        for i in (1, 2):
+            for side in range(2):
+                y_step(i, side, r).wait_recv()
+
+        def add_y(b, carry):
+            total = part[k, y, b, rows].astype(F32) + r1[y, b, rows].astype(F32)
+            total = total + r2[1, b, rows].astype(F32) + r2[2, b, rows].astype(F32)
+            s2[b, rows] = total.astype(BF16)
             return carry
 
-        lax.fori_loop(4 * side, 4 * side + 4, add_relayed, 0)
-        y_step(2, side).start()
-    core_step(3, k).wait_recv()
-    for i in (1, 2):
-        for side in range(2):
-            y_step(i, side).wait_recv()
-    def add_y(b, carry):
-        total = part[k, y, b].astype(F32) + r1[y, b].astype(F32) + r2[1, b].astype(F32) + r2[2, b].astype(F32)
-        s2[b] = total.astype(BF16)
-        return carry
-
-    lax.fori_loop(0, 8, add_y, 0)
-
-    def z_step(i):
-        to = lax.rem(z + i, 8)
-        return copy(s2.at[to], r3.at[i - 1], r3_send.at[i - 1], r3_recv.at[i - 1], S, y * 16 + to * 2 + k)
-
-    for i in range(1, 8):
-        z_step(i).start()
-    for i in range(1, 8):
-        z_step(i).wait_recv()
+        lax.fori_loop(0, 8, add_y, 0)
+        for d in range(7, 0, -1):
+            @pl.when(z + d < 8)
+            def _():
+                z_step(d, r).start()
+
+            @pl.when(z >= d)
+            def _():
+                z_step(8 - d, r).start()
+
+    for r in range(2):
+        for i in range(1, 8):
+            z_step(i, r).wait_recv()
 
     total = s2[z].astype(F32)
     for i in range(7):
@@ -605,9 +634,11 @@
         core_step(i, 1 - k).wait_send()
     for i in range(3):
         for side in range(2):
-            y_step(i, side).wait_send()
+            for r in range(2):
+                y_step(i, side, r).wait_send()
     for i in range(1, 8):
-        z_step(i).wait_send()
+        for r in range(2):
+            z_step(i, r).wait_send()
     @each
     def _(c):
         x_chunk(x, c, near, 0).wait_send()
@@ -710,10 +741,10 @@
             sem,
             sem((4,)),
             sem((4,)),
-            sem((3, 2)),
-            sem((3, 2)),
-            sem((7,)),
-            sem((7,)),
+            sem((3, 2, 2)),
+            sem((3, 2, 2)),
+            sem((7, 2)),
+            sem((7, 2)),
             sem((2,)),
             pltpu.SemaphoreType.REGULAR,
             pltpu.SemaphoreType.REGULAR,

time: 80.9 us -> 80.8 us (level)
  no operation moved by 1% of the time
where the time goes in v10:
time: 80.8 us; the launch traced here: 80.6 us
  Pallas kernels  77.2 us (96%)
  local copies, waits for them, and re-layouts  2.76 us (3%)
    pallas_call x1, Pallas kernels, body(): pl.pallas_call(functools.partial(kernel, scale), out_shape=(jax.ShapeDtyp...  77.2 us
    unnamed x2, local copies, waits for them, and re-layouts  2.76 us

profile of v10, /device:TPU:1, one launch (start us, length us, event | category | flops | bytes accessed | tf_op | source)
XLA Modules:
  0.0 80.6 jit_solution(1382947748088139224)
XLA Ops:
  0.6 77.2 %window.1 = (f32[36,256]{1,0:T(8,128)}, f32[12,256]{1,0:T(8,128)}) custom-call(bf16[2,128,256]{2,1,0:T(8,128)(2,1)} %bitcast.8, bf16[2,128,256]{2,1,0:T(8,128)(2,1)} %bitcast.9, bf16[2304,256]{1,0:T(8,128)(2,1)} %bitcast.6, bf16[768,256]{1,0:T(8,128)(2,1)} %bitcast.7), custom_call_target="tpu_custom_call" | custom-call | tf_op jit(solution)/shard_map/window/pallas_call | solution.py:696
  77.8 1.4 %copy.6 = f32[1,36,256]{2,0,1:T(1,128)} copy(f32[1,36,256]{2,1,0:T(8,128)} %bitcast.10) | data formatting | bytes 73728
  79.3 1.3 %copy.7 = f32[1,12,256]{2,0,1:T(1,128)} copy(f32[1,12,256]{2,1,0:T(8,128)} %bitcast.11) | data formatting | bytes 24576

commit v11 on v10

--- a/solution.py
+++ b/solution.py
@@ -295,6 +295,7 @@
         def _():
             meet_line()
             cot_copy.start()
+            lax.fori_loop(9, 12, lambda n, carry: turn(x, n), 0)
 
     def rows_of(c, h):
         return pl.ds(pl.multiple_of(h * 128 + c * HALF, HALF), HALF)
@@ -377,6 +378,7 @@
         @pl.when(x < 3)
         def _():
             meet_line()
+            lax.fori_loop(9, 12, lambda n, carry: turn(x, n), 0)
 
     def x_copy(j):
         return copy(bx.at[j], xin.at[mine], bx_send.at[j], x_recv.at[mine], base + j, D)
@@ -436,7 +438,7 @@
 
         @pl.when(half == 0)
         def _():
-            lax.fori_loop(12, 48, lambda n, carry: turn(n // 12, n % 12), 0)
+            lax.fori_loop(0, 48, lambda n, carry: turn(n // 12, n % 12), 0)
             back_copy.wait_recv()
 
         @pl.when(half == 1)
@@ -503,7 +505,7 @@
 
         keep(gb, c, gin[c])
         g = gin[c].astype(F32)
-        keep(gp, c, (g_hidden_of(g, wv.at[x]) * act[c]).astype(BF16))
+        keep(gp, c, (g_hidden_turned(g, turned.at[x]) * act[c]).astype(BF16))
         return carry
 
     lax.fori_loop(0, 2, clip_back, 0)

time: 80.8 us -> 80.8 us (level)
  no operation moved by 1% of the time
where the time goes in v11:
time: 80.8 us; the launch traced here: 80.6 us
  Pallas kernels  77.2 us (96%)
  local copies, waits for them, and re-layouts  2.76 us (3%)
    pallas_call x1, Pallas kernels, body(): pl.pallas_call(functools.partial(kernel, scale), out_shape=(jax.ShapeDtyp...  77.2 us
    unnamed x2, local copies, waits for them, and re-layouts  2.76 us

profile of v11, /device:TPU:1, one launch (start us, length us, event | category | flops | bytes accessed | tf_op | source)
XLA Modules:
  0.0 80.6 jit_solution(18293691770331797315)
XLA Ops:
  0.6 77.2 %window.1 = (f32[36,256]{1,0:T(8,128)}, f32[12,256]{1,0:T(8,128)}) custom-call(bf16[2,128,256]{2,1,0:T(8,128)(2,1)} %bitcast.8, bf16[2,128,256]{2,1,0:T(8,128)(2,1)} %bitcast.9, bf16[2304,256]{1,0:T(8,128)(2,1)} %bitcast.6, bf16[768,256]{1,0:T(8,128)(2,1)} %bitcast.7), custom_call_target="tpu_custom_call" | custom-call | tf_op jit(solution)/shard_map/window/pallas_call | solution.py:698
  77.8 1.4 %copy.6 = f32[1,36,256]{2,0,1:T(1,128)} copy(f32[1,36,256]{2,1,0:T(8,128)} %bitcast.10) | data formatting | bytes 73728
  79.2 1.3 %copy.7 = f32[1,12,256]{2,0,1:T(1,128)} copy(f32[1,12,256]{2,1,0:T(8,128)} %bitcast.11) | data formatting | bytes 24576
